TPU v7x, 512 devices: a whole 4x4x16 slice. The times are simulated.
512 devices in a mesh: rows: 16 (over z), tm: 32 (over x, y, core).
Axes of the slice: x: 4, y: 4, z: 16, core: 2. Of those that a mesh axis runs over, the one named last changes fastest.
Arguments:
- jacobian: bfloat16 [64, 6144, 512], P('tm', 'rows'), may hold values from -3 to 3
- rhs: bfloat16 [64, 6144], P('tm', 'rows'), may hold values from -6 to 6
- forget: float32 [64], P('tm'), may hold values from 0.99 to 1
- restart: int32 [64], P('tm'), may hold values 0 or 1
Outputs:
- factor: float32 [64, 512, 512], P('tm', 'rows')
- state: float32 [64, 512], P('tm', 'rows')
All inputs are finite; a program needn't handle non-finite values. No bound on the sum of `restart` on one device may be relied on, other than what follows from the above.
Results may differ from a plain program's by a relative error of at most 0.0003.
Values sent between devices are 32-bit elements; how exact they have to be, the bound alone decides.
No kernel may reach another device: no remote copies, remote signals or barrier semaphores. Data moves between devices by JAX's collectives and lax.ppermute only.
A program may use at most 128 MiB of HBM per device.

v0:
```python
import jax
import jax.numpy as jnp
from jax import lax
from jax.sharding import PartitionSpec as P


def prefix(value, axis, join, neutral):
    count, mine = (lax.axis_size(axis), lax.axis_index(axis))
    pieces = jax.tree.map(lambda part: lax.all_gather(part, axis), value)
    total = jax.tree.map(
        lambda part, zero: jnp.full_like(part, 0) + jnp.asarray(zero, part.dtype), value, neutral
    )

    def turn(position, total):
        longer = join(total, jax.tree.map(lambda part: part[position], pieces))
        return jax.tree.map(lambda new, old: jnp.where(position < mine, new, old), longer, total)

    return lax.fori_loop(0, count - 1, turn, total)


def chain_join(earlier, later_part):
    return (
        earlier[0] * later_part[0],
        later_part[0] * earlier[1] + later_part[1],
        later_part[0] * earlier[2] + later_part[2],
    )


def running(matrices, vectors, decays):
    matrix_now = jnp.zeros_like(matrices[0])
    vector_now = jnp.zeros_like(vectors[0])
    retained = jnp.float32(1.0)
    local_mats, local_vecs, retain_list = ([], [], [])
    for position in range(len(matrices)):
        matrix_now = decays[position] * matrix_now + matrices[position]
        vector_now = decays[position] * vector_now + vectors[position]
        retained = retained * decays[position]
        local_mats.append(matrix_now)
        local_vecs.append(vector_now)
        retain_list.append(retained)
    return (local_mats, local_vecs, retain_list)


def solve_rows(matrix, vector, row_start, row_share):
    lower_factor = jnp.linalg.cholesky(matrix)
    middle = jax.scipy.linalg.solve_triangular(lower_factor, vector, lower=True)
    result = jax.scipy.linalg.solve_triangular(lower_factor, middle, lower=True, trans=1)
    upper_rows = lax.dynamic_slice_in_dim(lower_factor.T, row_start, row_share, 0)
    result_rows = lax.dynamic_slice_in_dim(result, row_start, row_share, 0)
    return (upper_rows, result_rows)


def on_device(jacobian, rhs, forget, restart):
    segments_here = jacobian.shape[0]
    state_width = jacobian.shape[2]
    row_share = state_width // lax.axis_size("rows")
    row_start = lax.axis_index("rows") * row_share
    decays = forget * (1.0 - 0.2 * restart.astype(jnp.float32))
    partial_value = jnp.einsum(
        "srv,srw->svw", jacobian, jacobian, preferred_element_type=jnp.float32
    )
    gradient = jnp.einsum("sr,srv->sv", rhs, jacobian, preferred_element_type=jnp.float32)
    information, projected = lax.psum((partial_value, gradient), "rows")
    matrices = [information[position] for position in range(segments_here)]
    vectors = [projected[position] for position in range(segments_here)]
    local_mats, local_vecs, retain_list = running(matrices, vectors, decays)
    identity = (jnp.float32(1.0), jnp.zeros_like(local_mats[0]), jnp.zeros_like(local_vecs[0]))
    before = prefix((retain_list[-1], local_mats[-1], local_vecs[-1]), "tm", chain_join, identity)
    pieces = [
        solve_rows(
            retain_list[p] * before[1] + local_mats[p],
            retain_list[p] * before[2] + local_vecs[p],
            row_start,
            row_share,
        )
        for p in range(segments_here)
    ]
    factor = jnp.stack([piece[0] for piece in pieces], axis=0)
    state = jnp.stack([piece[1] for piece in pieces], axis=0)
    return (factor, state)


def solution(mesh):
    in_specs = (P("tm", "rows", None), P("tm", "rows"), P("tm"), P("tm"))
    out_specs = (P("tm", "rows", None), P("tm", "rows"))
    return jax.shard_map(
        on_device, mesh=mesh, in_specs=in_specs, out_specs=out_specs, check_vma=False
    )
```

profile of v0, /device:TPU:1, one launch (start us, length us, event | category | flops | bytes accessed | tf_op | source)
XLA Modules:
  0.0 704.6 jit_solution(4087259530837197838)
XLA Ops:
  11.7 139.7 %all-reduce.4.cloned.1.call-done = f32[2,512,512]{1,2,0:T(8,128)} async-done(((f32[2,512,512]{1,2,0:T(8,128)}), f32[2,512,512]{1,2,0:T(8,128)}) %all-reduce.4.cloned.1.call-update) | async-done | bytes 2097168 | tf_op jit(solution)/shard_map/psum | solution.py:63
  151.4 2.4 multiply_add_fusion
  156.6 21.5 %psum.15 = f32[2,512]{1,0:T(2,128)S(1)} all-reduce(f32[2,512]{1,0:T(2,128)S(1)} %bitcast.351), channel_id=1, replica_groups=mesh['rows'=16,'tm'=32] {'rows'}, use_global_device_ids=true, to_apply=%region_1.0 | all-reduce | flops 1024 | bytes 8192 | tf_op jit(solution)/shard_map/psum | solution.py:63
  178.8 41.1 %all-gather = f32[32,1,512]{2,1,0:T(1,128)S(1)} all-gather(f32[1,1,512]{2,1,0:T(1,128)S(1)} %get-tuple-element.231), channel_id=1, replica_groups=mesh['rows'=16,'tm'=32] {'tm'}, dimensions={0}, use_global_device_ids=true | all-gather | bytes 67584 | tf_op jit(solution)/shard_map/all_gather | solution.py:9
  222.0 63.8 %all-reduce.1 = f32[32]{0:T(128)S(1)} all-reduce(f32[32]{0:T(128)S(1)} %dynamic-update-slice.20), channel_id=1, replica_groups=mesh['rows'=16,'tm'=32] {'tm'}, use_global_device_ids=true, to_apply=%add.1 | all-reduce | flops 32 | bytes 256
  285.8 4.5 all-gather.3.cloned.1.call-done
  290.3 110.1 %while.24 = (s32[]{:T(128)}, f32[512,512]{1,0:T(8,128)S(1)}, f32[512]{0:T(512)S(1)}, s32[]{:T(128)}, f32[32]{0:T(128)S(1)}, /*index=5*/f32[32,512,512]{2,1,0:T(8,128)}, f32[32,512]{1,0:T(8,128)S(1)}, s32[]{:T(128)}, s32[]{:T(128)}) while((s32[]{:T(128)}, f32[512,512]{1,0:T(8,128)S(1)}, f32[512]{0:T(512)S(1)}, s32[]{:T(128)}, ...), condition=%wide.region_3.4_spmd.clone, body=%wide.region_2.3_spmd.clone.sunk | while | flops 1050628 | bytes 3156111 | solution.py:18
  294.4 2.3 fusion.142
  297.9 2.3 fusion.142
  301.5 2.3 fusion.142
  305.0 2.3 fusion.142
  312.1 2.3 fusion.142
  315.7 2.3 fusion.142
  319.2 2.3 fusion.142
  322.8 2.3 fusion.142
  329.9 2.3 fusion.142
  333.4 2.3 fusion.142
  336.9 2.3 fusion.142
  347.6 2.3 fusion.142
  351.1 2.3 fusion.142
  354.7 2.3 fusion.142
  361.8 2.3 fusion.142
  365.3 2.3 fusion.142
  368.9 2.3 fusion.142
  372.4 2.3 fusion.142
  379.5 2.3 fusion.142
  383.0 2.3 fusion.142
  386.6 2.3 fusion.142
  401.7 3.4 bitcast_add_fusion.4
  407.9 3.1 fusion.25
  411.9 11.7 %cholesky.286 = f32[128,128]{1,0:T(8,128)S(1)} custom-call(f32[128,128]{1,0:T(8,128)S(1)} %cholesky.426), custom_call_target="Cholesky" | custom-call | tf_op jit(solution)/shard_map/jit(cholesky)/cholesky | solution.py:45
  423.7 9.8 %custom-call.33 = f32[1,128,128]{1,2,0:T(8,128)S(1)} custom-call(f32[1,128,128]{2,1,0:T(8,128)S(1)} %get-tuple-element.248), custom_call_target="InvertDiagBlocksLowerTriangular" | custom-call | tf_op jit(solution)/shard_map/jit(cholesky)/cholesky | solution.py:45
  437.2 12.1 %cholesky.358 = f32[128,128]{1,0:T(8,128)S(1)} custom-call(f32[128,128]{1,0:T(8,128)S(1)} %cholesky.439), custom_call_target="Cholesky" | custom-call | tf_op jit(solution)/shard_map/jit(cholesky)/cholesky | solution.py:45
  449.4 9.8 %custom-call.36 = f32[1,128,128]{1,2,0:T(8,128)S(1)} custom-call(f32[1,128,128]{2,1,0:T(8,128)S(1)} %get-tuple-element.258), custom_call_target="InvertDiagBlocksLowerTriangular" | custom-call | tf_op jit(solution)/shard_map/jit(cholesky)/cholesky | solution.py:45
  462.2 11.7 %cholesky.305 = f32[128,128]{1,0:T(8,128)S(1)} custom-call(f32[128,128]{1,0:T(8,128)S(1)} %cholesky.430), custom_call_target="Cholesky" | custom-call | tf_op jit(solution)/shard_map/jit(cholesky)/cholesky | solution.py:45
  475.3 9.8 %custom-call.34 = f32[1,128,128]{1,2,0:T(8,128)S(1)} custom-call(f32[1,128,128]{2,1,0:T(8,128)S(1)} %get-tuple-element.245), custom_call_target="InvertDiagBlocksLowerTriangular" | custom-call | tf_op jit(solution)/shard_map/jit(cholesky)/cholesky | solution.py:45
  486.7 11.9 %cholesky.326 = f32[128,128]{1,0:T(8,128)S(1)} custom-call(f32[128,128]{1,0:T(8,128)S(1)} %cholesky.435), custom_call_target="Cholesky" | custom-call | tf_op jit(solution)/shard_map/jit(cholesky)/cholesky | solution.py:45
  499.3 9.8 %custom-call.35 = f32[1,128,128]{1,2,0:T(8,128)S(1)} custom-call(f32[1,128,128]{2,1,0:T(8,128)S(1)} %get-tuple-element.242), custom_call_target="InvertDiagBlocksLowerTriangular" | custom-call | tf_op jit(solution)/shard_map/jit(cholesky)/cholesky | solution.py:45
  510.5 11.7 %cholesky.343 = f32[128,128]{1,0:T(8,128)S(1)} custom-call(f32[128,128]{1,0:T(8,128)S(1)} %convolution_subtract_fusion.5), custom_call_target="Cholesky" | custom-call | tf_op jit(solution)/shard_map/jit(cholesky)/cholesky | solution.py:45
  526.8 7.9 %while.25 = (s32[]{:T(128)}, f32[512,512]{1,0:T(8,128)S(1)}, s32[4,2]{0,1:T(2,128)S(1)}, f32[4,128,128]{2,1,0:T(8,128)S(1)}, s32[]{:T(128)}) while((s32[]{:T(128)}, f32[512,512]{1,0:T(8,128)S(1)}, s32[4,2]{0,1:T(2,128)S(1)}, f32[4,128,128]{2,1,0:T(8,128)S(1)}, s32[]{:T(128)}) %tuple.103), condition=%wide.while_cond.1, body=%wide.while_body.1.sunk | while | flops 2 | bytes 131181 | solution.py:47
  534.7 39.5 %custom-call.40 = f32[4,128,128]{1,2,0:T(8,128)S(1)} custom-call(f32[4,128,128]{2,1,0:T(8,128)S(1)} %get-tuple-element.185), custom_call_target="InvertDiagBlocksLowerTriangular" | custom-call | tf_op jit(solution)/shard_map/jit(_solve_triangular)/triangular_solve | solution.py:47
  578.6 11.7 %cholesky.377 = f32[128,128]{1,0:T(8,128)S(1)} custom-call(f32[128,128]{1,0:T(8,128)S(1)} %cholesky.443), custom_call_target="Cholesky" | custom-call | tf_op jit(solution)/shard_map/jit(cholesky)/cholesky | solution.py:45
  591.7 9.8 %custom-call.37 = f32[1,128,128]{1,2,0:T(8,128)S(1)} custom-call(f32[1,128,128]{2,1,0:T(8,128)S(1)} %get-tuple-element.255), custom_call_target="InvertDiagBlocksLowerTriangular" | custom-call | tf_op jit(solution)/shard_map/jit(cholesky)/cholesky | solution.py:45
  603.0 11.7 %cholesky.398 = f32[128,128]{1,0:T(8,128)S(1)} custom-call(f32[128,128]{1,0:T(8,128)S(1)} %cholesky.448), custom_call_target="Cholesky" | custom-call | tf_op jit(solution)/shard_map/jit(cholesky)/cholesky | solution.py:45
  615.5 10.0 %custom-call.38 = f32[1,128,128]{1,2,0:T(8,128)S(1)} custom-call(f32[1,128,128]{2,1,0:T(8,128)S(1)} %get-tuple-element.252), custom_call_target="InvertDiagBlocksLowerTriangular" | custom-call | tf_op jit(solution)/shard_map/jit(cholesky)/cholesky | solution.py:45
  626.9 11.7 %cholesky.415 = f32[128,128]{1,0:T(8,128)S(1)} custom-call(f32[128,128]{1,0:T(8,128)S(1)} %convolution_subtract_fusion.4), custom_call_target="Cholesky" | custom-call | tf_op jit(solution)/shard_map/jit(cholesky)/cholesky | solution.py:45
  643.3 7.9 %while.26 = (s32[]{:T(128)}, f32[512,512]{1,0:T(8,128)S(1)}, s32[4,2]{0,1:T(2,128)S(1)}, f32[4,128,128]{2,1,0:T(8,128)S(1)}, s32[]{:T(128)}) while((s32[]{:T(128)}, f32[512,512]{1,0:T(8,128)S(1)}, s32[4,2]{0,1:T(2,128)S(1)}, f32[4,128,128]{2,1,0:T(8,128)S(1)}, s32[]{:T(128)}) %tuple.110), condition=%wide.while_cond.1.clone, body=%wide.while_body.1.clone.sunk | while | flops 2 | bytes 131181 | solution.py:47
  651.2 39.3 %custom-call.42 = f32[4,128,128]{1,2,0:T(8,128)S(1)} custom-call(f32[4,128,128]{2,1,0:T(8,128)S(1)} %get-tuple-element.187), custom_call_target="InvertDiagBlocksLowerTriangular" | custom-call | tf_op jit(solution)/shard_map/jit(_solve_triangular)/triangular_solve | solution.py:47
  (244 shorter events, 121.0 us)
Async XLA Ops:
  7.2 1.1 copy-start
  7.2 3.3 copy-start.3
  7.2 3.3 copy-start.4
  7.2 144.2 %all-reduce.4.cloned.1.call-start = ((), (), s32[]{:S(2)}) async-start(), calls=%async_computation | async-start | bytes 4194304 | tf_op jit(solution)/shard_map/psum | solution.py:63
  10.4 279.8 %all-gather.3.cloned.1.call-start = ((), (), s32[]{:S(2)}) async-start(), calls=%async_computation.1 | async-start | bytes 34603008 | tf_op jit(solution)/shard_map/all_gather | solution.py:9
  153.8 2.6 copy-start.2
  410.9 1.0 copy-start.1
Sparse Core Ops, SparseCore 0:
  10.5 140.8 all-reduce.3
  155.3 134.9 all-gather.2
where the time goes:
time: 710 us; the launch traced here: 705 us
  other arithmetic  343 us (48%)
  waiting for transfers between devices  144 us (20%)
  blocking collectives  126 us (18%)
  local copies, waits for them, and re-layouts  48.6 us (7%)
  between operations  21.9 us (3%)
  matrix products  19.5 us (3%)
    another operation x30, other arithmetic, solve_rows(): lower_factor = jnp.linalg.cholesky(matrix)  159 us
    psum x1, waiting for transfers between devices, on_device(): information, projected = lax.psum((partial_value, gradient), 'rows')  140 us
    select_n x62, other arithmetic, turn(): jnp.where(position < mine, new, old)  90.3 us
    another operation x7, other arithmetic, solve_rows(): jax.scipy.linalg.solve_triangular(lower_factor, middle, lower=True, trans=1)  81.4 us
    unnamed x1, blocking collectives  63.8 us
    all_gather x1, blocking collectives, prefix(): pieces = jax.tree.map(lambda part: lax.all_gather(part, axis), value)  41.1 us
    psum x1, blocking collectives, on_device(): information, projected = lax.psum((partial_value, gradient), 'rows')  21.5 us
    dynamic_slice x62, local copies, waits for them, and re-layouts, turn(): longer = join(total, jax.tree.map(lambda part: part[position], pieces))  18.7 us
  transfers between devices with their start and end apart: 2, of which 2 were waited for; matrix products, arithmetic and copies ran while one was open for 1% of the time, Pallas kernels for 0%

commit v1 on v0

v1 whole, which is shorter than its diff:
```python
import jax
import jax.numpy as jnp
from jax import lax
from jax.experimental import pallas as pl
from jax.experimental.pallas import tpu as pltpu
from jax.sharding import PartitionSpec as P

f32 = jnp.float32
B = 128
HIGH = lax.Precision.HIGHEST
VM = pl.BlockSpec(memory_space=pltpu.VMEM)
SM = pl.BlockSpec(memory_space=pltpu.SMEM)
PARAMS = pltpu.CompilerParams(vmem_limit_bytes=48 << 20)


def block_list(nb):
    return [(b, c) for b in range(nb) for c in range(b, nb)]


def tile_array(*lead):
    return jax.ShapeDtypeStruct(tuple(lead) + (8, B), f32)


def pack_kernel(z_ref, jac_ref, rhs_ref, own, up, down, up2, down2, parts):
    z = z_ref[0]
    segs, rows, width = jac_ref.shape
    nb = width // B
    blocks = block_list(nb)
    last = segs * len(blocks)
    for p in range(4):
        for a in range(4):
            parts[p, a, last] = jnp.zeros((8, B), f32)
    grads = []
    for s in range(segs):
        jac = jac_ref[s]
        for b in range(nb):
            info = lax.dot_general(
                jac[:, b * B:(b + 1) * B], jac[:, b * B:],
                (((0,), (0,)), ((), ())), preferred_element_type=f32)
            for c in range(b, nb):
                tile = s * len(blocks) + blocks.index((b, c))
                piece = info[:, (c - b) * B:(c - b + 1) * B].reshape(4, 4, 8, B)
                for q in range(4):
                    p = lax.rem(q + 16 - z, 4)
                    for a in range(4):
                        parts[p, a, tile] = piece[a, q]
        grads.append(jnp.dot(rhs_ref[...], jac, preferred_element_type=f32)[s:s + 1])
    p = lax.rem(16 - z, 4)
    for s in range(segs):
        for b in range(nb):
            parts[p, 0, last, pl.ds(s * nb + b, 1), :] = grads[s][:, b * B:(b + 1) * B]
    own[...] = parts[0]
    up[...] = parts[1]
    up2[...] = parts[2, 0:2]
    down2[...] = parts[2, 2:4]
    down[...] = parts[3]


def first_sum_kernel(z_ref, own, up, down, up2, down2, mine, plus, minus, far, total):
    h = lax.div(z_ref[0], 4)
    near = own[...] + up[...] + down[...]
    total[0:2] = near[0:2] + up2[...]
    total[2:4] = near[2:4] + down2[...]
    mine[...] = total[h]
    plus[...] = total[lax.rem(h + 1, 4)]
    minus[...] = total[lax.rem(h + 3, 4)]
    far[...] = total[lax.rem(h + 2, 4)]


def second_sum_kernel(decay_ref, mine, plus, minus, far, out, flat):
    total = (mine[...] + plus[...]) + (minus[...] + far[...])
    half = (total.shape[0] - 1) // 2
    for s in range(2):
        flat[s, 0:8 * half] = total[s * half:(s + 1) * half].reshape(8 * half, B)
        flat[s, 8 * half:8 * half + 4] = total[2 * half, 4 * s:4 * s + 4]
        flat[s, 8 * half + 4:] = jnp.zeros((flat.shape[1] - 8 * half - 4, B), f32)
    for t in range(out.shape[0]):
        for s in range(2):
            out[t, 3 * s:3 * s + 3] = flat[s, 3 * t:3 * t + 3]
            out[t, 6 + s:7 + s] = jnp.full((1, B), decay_ref[s], f32)


def scan_kernel(chunks, out):
    now = jnp.zeros((3, B), f32)
    for t in range(chunks.shape[0]):
        for s in range(2):
            now = chunks[t, 6 + s:7 + s] * now + chunks[t, 3 * s:3 * s + 3]
            out[t, 3 * s:3 * s + 3] = now
        out[t, 6:8] = jnp.zeros((2, B), f32)


def unpack_kernel(chunks, out, flat):
    half = (out.shape[0] - 1) // 2
    for t in range(chunks.shape[0]):
        for s in range(2):
            flat[s, 3 * t:3 * t + 3] = chunks[t, 3 * s:3 * s + 3]
    for s in range(2):
        out[s * half:(s + 1) * half] = flat[s, 0:8 * half].reshape(half, 8, B)
        out[2 * half, 4 * s:4 * s + 4] = flat[s, 8 * half:8 * half + 4]


def stack_kernel(mine, below, above, far, full, low, high):
    full[0] = below[...]
    full[1] = mine[...]
    full[2] = above[...]
    full[3] = far[...]
    low[0] = below[...]
    low[1] = mine[...]
    high[0] = mine[...]
    high[1] = above[...]


def spread(row):
    return jnp.broadcast_to(row, (8, B))


def invert_factor(rows, lane, sub):
    groups = len(rows)
    for j in range(groups):
        o = 8 * j
        top = rows[j]
        cols = [jnp.broadcast_to(top[:, o + m:o + m + 1], (8, B)) for m in range(8)]
        inside = (lane >= o) & (lane < o + 8)
        d = []
        for m in range(8):
            unit = jnp.where(lane == o + m, 1.0, 0.0)
            d.append(jnp.where(inside, unit, spread(top[m:m + 1])))
        low = {}
        rs = []
        u = []
        for k in range(8):
            r = lax.rsqrt(spread(cols[k][k:k + 1]))
            rs.append(r)
            col = cols[k] * r
            u.append(d[k] * r)
            for m in range(k + 1, 8):
                low[m, k] = spread(col[m:m + 1])
                cols[m] = cols[m] - col * low[m, k]
                d[m] = d[m] - low[m, k] * u[k]
        w = [None] * 8
        for m in range(7, -1, -1):
            acc = u[m]
            for k in range(m + 1, 8):
                acc = acc - low[k, m] * w[k]
            w[m] = acc * rs[m]
        for i in range(j + 1, groups):
            old = rows[i]
            new = jnp.where(inside, 0.0, old)
            for m in range(8):
                new = new - jnp.broadcast_to(old[:, o + m:o + m + 1], (8, B)) * w[m]
            rows[i] = new
        merged = u[0]
        for m in range(1, 8):
            merged = jnp.where(sub == m, u[m], merged)
        rows[j] = merged
    return rows


def solve_kernel(z_ref, own, up, down, up2, down2, factor, state, mat, upper, inv, vec, sol):
    z = z_ref[0]
    segs, width = mat.shape[0], mat.shape[1]
    nb = width // B
    blocks = block_list(nb)
    nblk = len(blocks)
    lane = lax.broadcasted_iota(jnp.int32, (8, B), 1)
    sub = lax.broadcasted_iota(jnp.int32, (8, B), 0)
    row_i = lax.broadcasted_iota(jnp.int32, (B, B), 0)
    col_i = lax.broadcasted_iota(jnp.int32, (B, B), 1)
    row_w = lax.broadcasted_iota(jnp.int32, (B, width), 0)
    col_w = lax.broadcasted_iota(jnp.int32, (B, width), 1)
    mat[...] = jnp.zeros(mat.shape, f32)
    vec[...] = jnp.zeros(vec.shape, f32)
    sol[...] = jnp.zeros(sol.shape, f32)

    def place(piece, source, shift):
        g = lax.rem(z + (source + shift + 32), 16)
        for s in range(segs):
            for i, (b, c) in enumerate(blocks):
                at = pl.multiple_of(b * B + g * 8, 8)
                mat[s, pl.ds(at, 8), c * B:(c + 1) * B] = piece[s * nblk + i]

        @pl.when(g == 0)
        def _():
            for s in range(segs):
                for b in range(nb):
                    vec[s, 0:1, b * B:(b + 1) * B] = piece[segs * nblk, s * nb + b:s * nb + b + 1]

    shifts = (-4, 0, 4, 8)
    for ref, source in ((own, 0), (up, -1), (down, 1)):
        for i in range(4):
            place(ref.at[i], source, shifts[i])
    for i in range(2):
        place(up2.at[i], -2, (-4, 0)[i])
        place(down2.at[i], 2, (0, 4)[i])

    def step(b, carry):
        at = pl.multiple_of(b * B, B)
        groups = B // 8
        found = []
        for s in range(segs):
            diag = mat[s, pl.ds(at, B), pl.ds(at, B)]
            found.append([diag[8 * i:8 * i + 8] for i in range(groups)])
        for s in range(segs):
            rows = invert_factor(found[s], lane, sub)
            full = jnp.concatenate(rows, axis=0)
            inv[s, b] = jnp.where(col_i <= row_i, full, 0.0)
        for s in range(segs):
            left = inv[s, b]
            panel = jnp.dot(left, mat[s, pl.ds(at, B), :], precision=HIGH, preferred_element_type=f32)
            panel = jnp.where(col_w >= row_w + at, panel, 0.0)
            upper[s, pl.ds(at, B), :] = panel
            y = lax.dot_general(vec[s, :, pl.ds(at, B)], left, (((1,), (1,)), ((), ())),
                                precision=HIGH, preferred_element_type=f32)
            sol[s, :, pl.ds(at, B)] = y
            vec[s] = vec[s] - jnp.dot(y, panel, precision=HIGH, preferred_element_type=f32)
            mat[s] = mat[s] - lax.dot_general(panel, panel, (((0,), (0,)), ((), ())),
                                              precision=HIGH, preferred_element_type=f32)
        return carry

    lax.fori_loop(0, nb, step, 0)

    vec[...] = jnp.zeros(vec.shape, f32)
    for b in range(nb - 1, -1, -1):
        for s in range(segs):
            y = sol[s, :, b * B:(b + 1) * B]
            if b < nb - 1:
                y = y - lax.dot_general(
                    vec[s, :, (b + 1) * B:], upper[s, b * B:(b + 1) * B, (b + 1) * B:],
                    (((1,), (1,)), ((), ())), precision=HIGH, preferred_element_type=f32)
            vec[s, :, b * B:(b + 1) * B] = jnp.dot(y, inv[s, b], precision=HIGH, preferred_element_type=f32)
    share = factor.shape[1]
    start = pl.multiple_of(z * share, share)
    for s in range(segs):
        factor[s] = upper[s, pl.ds(start, share), :]
        state[s:s + 1, :] = vec[s, 0:1, :]


def shifted(value, by):
    count = lax.axis_size("rows")
    return lax.ppermute(value, "rows", [(i, (i + by) % count) for i in range(count)])


def on_device(jacobian, rhs, forget, restart):
    segs, rows, width = jacobian.shape
    nb = width // B
    tiles = segs * len(block_list(nb)) + 1
    tms = lax.axis_size("tm")
    z = lax.axis_index("rows")
    z_now = z.astype(jnp.int32).reshape(1)
    share = width // lax.axis_size("rows")
    decays = forget * (1.0 - 0.2 * restart.astype(f32))

    four, two, one = tile_array(4, tiles), tile_array(2, tiles), tile_array(tiles)
    own, up, down, up2, down2 = pl.pallas_call(
        pack_kernel, out_shape=[four, four, four, two, two],
        in_specs=[SM, VM, VM], out_specs=[VM] * 5,
        scratch_shapes=[pltpu.VMEM((4, 4, tiles, 8, B), f32)],
        compiler_params=PARAMS, name="pack")(z_now, jacobian, rhs)
    up, down, up2, down2 = shifted(up, 1), shifted(down, -1), shifted(up2, 2), shifted(down2, -2)
    mine, plus, minus, far = pl.pallas_call(
        first_sum_kernel, out_shape=[one] * 4,
        in_specs=[SM] + [VM] * 5, out_specs=[VM] * 4,
        scratch_shapes=[pltpu.VMEM((4, tiles, 8, B), f32)],
        compiler_params=PARAMS, name="first_sum")(z_now, own, up, down, up2, down2)
    plus, minus, far = shifted(plus, 4), shifted(minus, -4), shifted(far, 8)
    chunks = pl.pallas_call(
        second_sum_kernel, out_shape=tile_array(tms),
        in_specs=[SM] + [VM] * 4, out_specs=VM,
        scratch_shapes=[pltpu.VMEM((2, 3 * tms, B), f32)],
        compiler_params=PARAMS, name="second_sum")(decays, mine, plus, minus, far)
    chunks = lax.all_to_all(chunks, "tm", 0, 0)
    chunks = pl.pallas_call(
        scan_kernel, out_shape=tile_array(tms), in_specs=[VM], out_specs=VM,
        compiler_params=PARAMS, name="scan")(chunks)
    chunks = lax.all_to_all(chunks, "tm", 0, 0)
    mine = pl.pallas_call(
        unpack_kernel, out_shape=one, in_specs=[VM], out_specs=VM,
        scratch_shapes=[pltpu.VMEM((2, 3 * tms, B), f32)],
        compiler_params=PARAMS, name="unpack")(chunks)
    below, above, far = shifted(mine, 4), shifted(mine, -4), shifted(mine, 8)
    own, low, high = pl.pallas_call(
        stack_kernel, out_shape=[four, two, two], in_specs=[VM] * 4, out_specs=[VM] * 3,
        compiler_params=PARAMS, name="stack")(mine, below, above, far)
    up, down, up2, down2 = shifted(own, 1), shifted(own, -1), shifted(low, 2), shifted(high, -2)
    factor, state = pl.pallas_call(
        solve_kernel,
        out_shape=[jax.ShapeDtypeStruct((segs, share, width), f32), jax.ShapeDtypeStruct((segs, width), f32)],
        in_specs=[SM] + [VM] * 5, out_specs=[VM] * 2,
        scratch_shapes=[
            pltpu.VMEM((segs, width, width), f32), pltpu.VMEM((segs, width, width), f32),
            pltpu.VMEM((segs, nb, B, B), f32), pltpu.VMEM((segs, 8, width), f32),
            pltpu.VMEM((segs, 8, width), f32)],
        compiler_params=PARAMS, name="solve")(z_now, own, up, down, up2, down2)
    return (factor, lax.dynamic_slice_in_dim(state, z * share, share, 1))


def solution(mesh):
    in_specs = (P("tm", "rows", None), P("tm", "rows"), P("tm"), P("tm"))
    out_specs = (P("tm", "rows", None), P("tm", "rows"))
    return jax.shard_map(
        on_device, mesh=mesh, in_specs=in_specs, out_specs=out_specs, check_vma=False
    )
```

time: 710 us -> 197 us (0.28)
  other arithmetic: 343 us -> 0.01 us
  waiting for transfers between devices: 144 us -> 26.1 us
  blocking collectives: 126 us -> 29.6 us
  starting transfers between devices: 0.08 us -> 80.6 us
  Pallas kernels: 0 us -> 56.5 us
  local copies, waits for them, and re-layouts: 48.6 us -> 2.45 us
  between operations: 21.9 us -> 0.84 us
  matrix products: 19.5 us -> 0 us
    another operation x41 -> x0, other arithmetic: 242 us -> none  [the longest x30 159 us: solve_rows(): lower_factor = jnp.linalg.cholesky(matrix)]
    psum x1 -> x0, waiting for transfers between devices: 140 us -> none  [on_device(): information, projected = lax.psum((partial_value, gradient), 'rows')]
    select_n x62 -> x0, other arithmetic: 90.3 us -> none  [turn(): jnp.where(position < mine, new, old)]
    ppermute x0 -> x14, starting transfers between devices: none -> 80.6 us  [shifted(): lax.ppermute(value, 'rows', [(i, (i + by) % count) for i in range(count)])]
    unnamed x1 -> x0, blocking collectives: 63.8 us -> none
    pallas_call x0 -> x7, Pallas kernels: none -> 56.5 us  [the longest x1 54.7 us: on_device(): pl.pallas_call(solve_kernel, out_shape=[jax.ShapeDtypeStruct((segs, share...]
    all_gather x1 -> x0, blocking collectives: 41.1 us -> none  [prefix(): pieces = jax.tree.map(lambda part: lax.all_gather(part, axis), value)]
    all_to_all x0 -> x2, blocking collectives: none -> 29.6 us  [on_device(): chunks = lax.all_to_all(chunks, 'tm', 0, 0)]
  transfers between devices with their start and end apart: 2 -> 14, of which waited for: 2 -> 7; matrix products, arithmetic and copies ran while one was open for 1% -> 0% of each run, Pallas kernels for 0% -> 0%
where the time goes in v1:
time: 197 us; the launch traced here: 196 us
  starting transfers between devices  80.6 us (41%)
  Pallas kernels  56.5 us (29%)
  blocking collectives  29.6 us (15%)
  waiting for transfers between devices  26.1 us (13%)
  local copies, waits for them, and re-layouts  2.45 us (1%)
    ppermute x14, starting transfers between devices, shifted(): lax.ppermute(value, 'rows', [(i, (i + by) % count) for i in range(count)])  80.6 us
    pallas_call x1, Pallas kernels, on_device(): pl.pallas_call(solve_kernel, out_shape=[jax.ShapeDtypeStruct((segs, share...  54.7 us
    all_to_all x2, blocking collectives, on_device(): chunks = lax.all_to_all(chunks, 'tm', 0, 0)  29.6 us
    ppermute x14, waiting for transfers between devices, shifted(): lax.ppermute(value, 'rows', [(i, (i + by) % count) for i in range(count)])  26.1 us
  transfers between devices with their start and end apart: 14, of which 7 were waited for; matrix products, arithmetic and copies ran while one was open for 0% of the time, Pallas kernels for 0%

profile of v1, /device:TPU:1, one launch (start us, length us, event | category | flops | bytes accessed | tf_op | source)
XLA Modules:
  0.0 196.0 jit_solution(3388274885225502057)
XLA Ops:
  0.6 0.0 copy-start.1
  0.6 0.7 copy-done.1
  1.3 0.0 copy-start
  1.3 1.1 copy-done
  2.4 0.9 pack.1
  3.3 4.4 %collective-permute-start = (f32[4,21,8,128]{3,2,1,0:T(8,128)S(1)}, f32[4,21,8,128]{3,2,1,0:T(8,128)S(1)}, u32[]{:S(2)}, u32[]{:S(2)}) collective-permute-start(f32[4,21,8,128]{3,2,1,0:T(8,128)S(1)} %get-tuple-element.17), channel_id=1, source_target_pairs={{0,32},{32,64},{64,96},{96,128},{128,160},{160,192},{192,224},{224... | collective-permute-start | bytes 1032200 | tf_op jit(solution)/shard_map/ppermute | solution.py:240
  7.7 9.5 %collective-permute-start.1 = (f32[4,21,8,128]{3,2,1,0:T(8,128)S(1)}, f32[4,21,8,128]{3,2,1,0:T(8,128)S(1)}, u32[]{:S(2)}, u32[]{:S(2)}) collective-permute-start(f32[4,21,8,128]{3,2,1,0:T(8,128)S(1)} %get-tuple-element.18), channel_id=1, source_target_pairs={{0,480},{32,0},{64,32},{96,64},{128,96},{160,128},{192,160},{224,1... | collective-permute-start | bytes 1032200 | tf_op jit(solution)/shard_map/ppermute | solution.py:240
  17.2 1.9 collective-permute-start.2
  19.2 5.5 %collective-permute-start.3 = (f32[2,21,8,128]{3,2,1,0:T(8,128)S(1)}, f32[2,21,8,128]{3,2,1,0:T(8,128)S(1)}, u32[]{:S(2)}, u32[]{:S(2)}) collective-permute-start(f32[2,21,8,128]{3,2,1,0:T(8,128)S(1)} %get-tuple-element.20), channel_id=1, source_target_pairs={{0,448},{32,480},{64,0},{96,32},{128,64},{160,96},{192,128},{224,1... | collective-permute-start | bytes 516104 | tf_op jit(solution)/shard_map/ppermute | solution.py:240
  24.6 4.6 %collective-permute-done.2.up2 = f32[2,21,8,128]{3,2,1,0:T(8,128)S(1)} collective-permute-done((f32[2,21,8,128]{3,2,1,0:T(8,128)S(1)}, f32[2,21,8,128]{3,2,1,0:T(8,128)S(1)}, u32[]{:S(2)}, u32[]{:S(2)}) %collective-permute-start.2) | collective-permute-done | bytes 172064 | tf_op jit(solution)/shard_map/ppermute | solution.py:240
  29.3 1.8 collective-permute-done.3.down2
  31.1 0.0 collective-permute-done.up
  31.1 0.0 collective-permute-done.1.down
  31.1 0.1 first_sum.1
  31.2 6.9 %collective-permute-start.4 = (f32[21,8,128]{2,1,0:T(8,128)S(1)}, f32[21,8,128]{2,1,0:T(8,128)S(1)}, u32[]{:S(2)}, u32[]{:S(2)}) collective-permute-start(f32[21,8,128]{2,1,0:T(8,128)S(1)} %get-tuple-element.22), channel_id=1, source_target_pairs={{0,128},{32,160},{64,192},{96,224},{128,256},{160,288},{192,320},{... | collective-permute-start | bytes 258056 | tf_op jit(solution)/shard_map/ppermute | solution.py:240
  38.2 0.0 copy-start.2
  38.2 0.0 copy-start.3
  38.2 2.2 %collective-permute-start.5 = (f32[21,8,128]{2,1,0:T(8,128)S(1)}, f32[21,8,128]{2,1,0:T(8,128)S(1)}, u32[]{:S(2)}, u32[]{:S(2)}) collective-permute-start(f32[21,8,128]{2,1,0:T(8,128)S(1)} %get-tuple-element.23), channel_id=1, source_target_pairs={{0,384},{32,416},{64,448},{96,480},{128,0},{160,32},{192,64},{224,... | collective-permute-start | bytes 258056 | tf_op jit(solution)/shard_map/ppermute | solution.py:240
  40.5 10.1 %collective-permute-start.6 = (f32[21,8,128]{2,1,0:T(8,128)S(1)}, f32[21,8,128]{2,1,0:T(8,128)S(1)}, u32[]{:S(2)}, u32[]{:S(2)}) collective-permute-start(f32[21,8,128]{2,1,0:T(8,128)S(1)} %get-tuple-element.24), channel_id=1, source_target_pairs={{0,256},{32,288},{64,320},{96,352},{128,384},{160,416},{192,448},{... | collective-permute-start | bytes 258056 | tf_op jit(solution)/shard_map/ppermute | solution.py:240
  50.5 0.0 copy-done.2
  50.5 0.0 copy-done.3
  50.6 0.0 collective-permute-done.4.plus
  50.6 0.0 collective-permute-done.5.minus
  50.6 3.9 %collective-permute-done.6.far = f32[21,8,128]{2,1,0:T(8,128)S(1)} collective-permute-done((f32[21,8,128]{2,1,0:T(8,128)S(1)}, f32[21,8,128]{2,1,0:T(8,128)S(1)}, u32[]{:S(2)}, u32[]{:S(2)}) %collective-permute-start.6) | collective-permute-done | bytes 86048 | tf_op jit(solution)/shard_map/ppermute | solution.py:240
  54.5 0.6 second_sum.1
  55.1 18.3 %all_to_all.10.chunks = f32[32,8,128]{2,1,0:T(8,128)S(1)} all-to-all(f32[32,8,128]{2,1,0:T(8,128)S(1)} %second_sum.1), channel_id=1, replica_groups=mesh['rows'=16,'tm'=32] {'tm'}, dimensions={0} | all-to-all | bytes 262144 | tf_op jit(solution)/shard_map/all_to_all | solution.py:271
  73.4 0.1 scan.1
  73.5 11.3 %all_to_all.11.chunks = f32[32,8,128]{2,1,0:T(8,128)S(1)} all-to-all(f32[32,8,128]{2,1,0:T(8,128)S(1)} %scan.1), channel_id=1, replica_groups=mesh['rows'=16,'tm'=32] {'tm'}, dimensions={0} | all-to-all | bytes 262144 | tf_op jit(solution)/shard_map/all_to_all | solution.py:275
  84.8 9.1 %collective-permute-start.7 = (f32[21,8,128]{2,1,0:T(8,128)S(1)}, f32[21,8,128]{2,1,0:T(8,128)S(1)}, u32[]{:S(2)}, u32[]{:S(2)}) collective-permute-start(f32[21,8,128]{2,1,0:T(8,128)S(1)} %unpack.1.mine), channel_id=1, source_target_pairs={{0,128},{32,160},{64,192},{96,224},{128,256},{160,288},{192,320},{... | collective-permute-start | bytes 258056 | tf_op jit(solution)/shard_map/ppermute | solution.py:240
  94.0 1.9 collective-permute-start.8
  95.9 9.3 %collective-permute-start.9 = (f32[21,8,128]{2,1,0:T(8,128)S(1)}, f32[21,8,128]{2,1,0:T(8,128)S(1)}, u32[]{:S(2)}, u32[]{:S(2)}) collective-permute-start(f32[21,8,128]{2,1,0:T(8,128)S(1)} %unpack.1.mine), channel_id=1, source_target_pairs={{0,256},{32,288},{64,320},{96,352},{128,384},{160,416},{192,448},{... | collective-permute-start | bytes 258056 | tf_op jit(solution)/shard_map/ppermute | solution.py:240
  105.2 0.0 collective-permute-done.7.below
  105.2 2.9 %collective-permute-done.8.above = f32[21,8,128]{2,1,0:T(8,128)S(1)} collective-permute-done((f32[21,8,128]{2,1,0:T(8,128)S(1)}, f32[21,8,128]{2,1,0:T(8,128)S(1)}, u32[]{:S(2)}, u32[]{:S(2)}) %collective-permute-start.8) | collective-permute-done | bytes 86048 | tf_op jit(solution)/shard_map/ppermute | solution.py:240
  108.1 1.8 collective-permute-done.9.far
  109.9 5.0 %collective-permute-start.10 = (f32[4,21,8,128]{3,2,1,0:T(8,128)S(1)}, f32[4,21,8,128]{3,2,1,0:T(8,128)S(1)}, u32[]{:S(2)}, u32[]{:S(2)}) collective-permute-start(f32[4,21,8,128]{3,2,1,0:T(8,128)S(1)} %get-tuple-element.25.own), channel_id=1, source_target_pairs={{0,32},{32,64},{64,96},{96,128},{128,160},{160,192},{192,224},{224... | collective-permute-start | bytes 1032200 | tf_op jit(solution)/shard_map/ppermute | solution.py:240
  115.0 4.4 %collective-permute-start.11 = (f32[4,21,8,128]{3,2,1,0:T(8,128)S(1)}, f32[4,21,8,128]{3,2,1,0:T(8,128)S(1)}, u32[]{:S(2)}, u32[]{:S(2)}) collective-permute-start(f32[4,21,8,128]{3,2,1,0:T(8,128)S(1)} %get-tuple-element.25.own), channel_id=1, source_target_pairs={{0,480},{32,0},{64,32},{96,64},{128,96},{160,128},{192,160},{224,1... | collective-permute-start | bytes 1032200 | tf_op jit(solution)/shard_map/ppermute | solution.py:240
  119.4 8.2 %collective-permute-start.12 = (f32[2,21,8,128]{3,2,1,0:T(8,128)S(1)}, f32[2,21,8,128]{3,2,1,0:T(8,128)S(1)}, u32[]{:S(2)}, u32[]{:S(2)}) collective-permute-start(f32[2,21,8,128]{3,2,1,0:T(8,128)S(1)} %get-tuple-element.26), channel_id=1, source_target_pairs={{0,64},{32,96},{64,128},{96,160},{128,192},{160,224},{192,256},{22... | collective-permute-start | bytes 516104 | tf_op jit(solution)/shard_map/ppermute | solution.py:240
  127.6 2.1 %collective-permute-start.13 = (f32[2,21,8,128]{3,2,1,0:T(8,128)S(1)}, f32[2,21,8,128]{3,2,1,0:T(8,128)S(1)}, u32[]{:S(2)}, u32[]{:S(2)}) collective-permute-start(f32[2,21,8,128]{3,2,1,0:T(8,128)S(1)} %get-tuple-element.27), channel_id=1, source_target_pairs={{0,448},{32,480},{64,0},{96,32},{128,64},{160,96},{192,128},{224,1... | collective-permute-start | bytes 516104 | tf_op jit(solution)/shard_map/ppermute | solution.py:240
  129.7 4.7 %collective-permute-done.12.up2 = f32[2,21,8,128]{3,2,1,0:T(8,128)S(1)} collective-permute-done((f32[2,21,8,128]{3,2,1,0:T(8,128)S(1)}, f32[2,21,8,128]{3,2,1,0:T(8,128)S(1)}, u32[]{:S(2)}, u32[]{:S(2)}) %collective-permute-start.12) | collective-permute-done | bytes 172064 | tf_op jit(solution)/shard_map/ppermute | solution.py:240
  134.5 6.2 %collective-permute-done.13.down2 = f32[2,21,8,128]{3,2,1,0:T(8,128)S(1)} collective-permute-done((f32[2,21,8,128]{3,2,1,0:T(8,128)S(1)}, f32[2,21,8,128]{3,2,1,0:T(8,128)S(1)}, u32[]{:S(2)}, u32[]{:S(2)}) %collective-permute-start.13) | collective-permute-done | bytes 172064 | tf_op jit(solution)/shard_map/ppermute | solution.py:240
  140.7 0.0 collective-permute-done.10.up
  140.7 0.0 collective-permute-done.11.down
  140.7 54.7 %solve.1 = (f32[2,32,512]{2,1,0:T(8,128)}, f32[2,512]{1,0:T(2,128)S(1)}) custom-call(s32[1]{0:T(128)} %bitcast.z_ref, f32[4,21,8,128]{3,2,1,0:T(8,128)S(1)} %get-tuple-element.25.own, f32[4,21,8,128]{3,2,1,0:T(8,128)S(1)} %collective-permute-done.10.up, f32[4,21,8,128]{3,2,1,0:T(8,128)S(1)} %collective-permute-done.11.down, ...), custom_call_target="tpu_custom_call" | custom-call | tf_op jit(solution)/shard_map/solve/pallas_call | solution.py:285
  195.4 0.6 constant_dynamic-slice_fusion
  (3 shorter events, 0.1 us)
Async XLA Ops:
  0.6 0.7 copy-start.1
  1.3 1.1 copy-start
  3.3 27.8 %collective-permute-start = (f32[4,21,8,128]{3,2,1,0:T(8,128)S(1)}, f32[4,21,8,128]{3,2,1,0:T(8,128)S(1)}, u32[]{:S(2)}, u32[]{:S(2)}) collective-permute-start(f32[4,21,8,128]{3,2,1,0:T(8,128)S(1)} %get-tuple-element.17), channel_id=1, source_target_pairs={{0,32},{32,64},{64,96},{96,128},{128,160},{160,192},{192,224},{224... | collective-permute-start | bytes 1032200 | tf_op jit(solution)/shard_map/ppermute | solution.py:240
  7.7 23.4 %collective-permute-start.1 = (f32[4,21,8,128]{3,2,1,0:T(8,128)S(1)}, f32[4,21,8,128]{3,2,1,0:T(8,128)S(1)}, u32[]{:S(2)}, u32[]{:S(2)}) collective-permute-start(f32[4,21,8,128]{3,2,1,0:T(8,128)S(1)} %get-tuple-element.18), channel_id=1, source_target_pairs={{0,480},{32,0},{64,32},{96,64},{128,96},{160,128},{192,160},{224,1... | collective-permute-start | bytes 1032200 | tf_op jit(solution)/shard_map/ppermute | solution.py:240
  17.2 12.0 %collective-permute-start.2 = (f32[2,21,8,128]{3,2,1,0:T(8,128)S(1)}, f32[2,21,8,128]{3,2,1,0:T(8,128)S(1)}, u32[]{:S(2)}, u32[]{:S(2)}) collective-permute-start(f32[2,21,8,128]{3,2,1,0:T(8,128)S(1)} %get-tuple-element.19), channel_id=1, source_target_pairs={{0,64},{32,96},{64,128},{96,160},{128,192},{160,224},{192,256},{22... | collective-permute-start | bytes 516104 | tf_op jit(solution)/shard_map/ppermute | solution.py:240
  19.2 11.9 %collective-permute-start.3 = (f32[2,21,8,128]{3,2,1,0:T(8,128)S(1)}, f32[2,21,8,128]{3,2,1,0:T(8,128)S(1)}, u32[]{:S(2)}, u32[]{:S(2)}) collective-permute-start(f32[2,21,8,128]{3,2,1,0:T(8,128)S(1)} %get-tuple-element.20), channel_id=1, source_target_pairs={{0,448},{32,480},{64,0},{96,32},{128,64},{160,96},{192,128},{224,1... | collective-permute-start | bytes 516104 | tf_op jit(solution)/shard_map/ppermute | solution.py:240
  31.2 19.3 %collective-permute-start.4 = (f32[21,8,128]{2,1,0:T(8,128)S(1)}, f32[21,8,128]{2,1,0:T(8,128)S(1)}, u32[]{:S(2)}, u32[]{:S(2)}) collective-permute-start(f32[21,8,128]{2,1,0:T(8,128)S(1)} %get-tuple-element.22), channel_id=1, source_target_pairs={{0,128},{32,160},{64,192},{96,224},{128,256},{160,288},{192,320},{... | collective-permute-start | bytes 258056 | tf_op jit(solution)/shard_map/ppermute | solution.py:240
  38.2 12.3 %copy-start.2 = (f32[2]{0:T(128)S(1)}, f32[2]{0:T(128)}, u32[]{:S(2)}) copy-start(f32[2]{0:T(128)} %param.6) | copy-start | bytes 28
  38.2 12.3 %copy-start.3 = (s32[2]{0:T(128)S(1)}, s32[2]{0:T(128)}, u32[]{:S(2)}) copy-start(s32[2]{0:T(128)} %param.7) | copy-start | bytes 28
  38.2 12.4 %collective-permute-start.5 = (f32[21,8,128]{2,1,0:T(8,128)S(1)}, f32[21,8,128]{2,1,0:T(8,128)S(1)}, u32[]{:S(2)}, u32[]{:S(2)}) collective-permute-start(f32[21,8,128]{2,1,0:T(8,128)S(1)} %get-tuple-element.23), channel_id=1, source_target_pairs={{0,384},{32,416},{64,448},{96,480},{128,0},{160,32},{192,64},{224,... | collective-permute-start | bytes 258056 | tf_op jit(solution)/shard_map/ppermute | solution.py:240
  40.5 14.0 %collective-permute-start.6 = (f32[21,8,128]{2,1,0:T(8,128)S(1)}, f32[21,8,128]{2,1,0:T(8,128)S(1)}, u32[]{:S(2)}, u32[]{:S(2)}) collective-permute-start(f32[21,8,128]{2,1,0:T(8,128)S(1)} %get-tuple-element.24), channel_id=1, source_target_pairs={{0,256},{32,288},{64,320},{96,352},{128,384},{160,416},{192,448},{... | collective-permute-start | bytes 258056 | tf_op jit(solution)/shard_map/ppermute | solution.py:240
  84.8 20.3 %collective-permute-start.7 = (f32[21,8,128]{2,1,0:T(8,128)S(1)}, f32[21,8,128]{2,1,0:T(8,128)S(1)}, u32[]{:S(2)}, u32[]{:S(2)}) collective-permute-start(f32[21,8,128]{2,1,0:T(8,128)S(1)} %unpack.1.mine), channel_id=1, source_target_pairs={{0,128},{32,160},{64,192},{96,224},{128,256},{160,288},{192,320},{... | collective-permute-start | bytes 258056 | tf_op jit(solution)/shard_map/ppermute | solution.py:240
  94.0 14.2 %collective-permute-start.8 = (f32[21,8,128]{2,1,0:T(8,128)S(1)}, f32[21,8,128]{2,1,0:T(8,128)S(1)}, u32[]{:S(2)}, u32[]{:S(2)}) collective-permute-start(f32[21,8,128]{2,1,0:T(8,128)S(1)} %unpack.1.mine), channel_id=1, source_target_pairs={{0,384},{32,416},{64,448},{96,480},{128,0},{160,32},{192,64},{224,... | collective-permute-start | bytes 258056 | tf_op jit(solution)/shard_map/ppermute | solution.py:240
  95.9 14.0 %collective-permute-start.9 = (f32[21,8,128]{2,1,0:T(8,128)S(1)}, f32[21,8,128]{2,1,0:T(8,128)S(1)}, u32[]{:S(2)}, u32[]{:S(2)}) collective-permute-start(f32[21,8,128]{2,1,0:T(8,128)S(1)} %unpack.1.mine), channel_id=1, source_target_pairs={{0,256},{32,288},{64,320},{96,352},{128,384},{160,416},{192,448},{... | collective-permute-start | bytes 258056 | tf_op jit(solution)/shard_map/ppermute | solution.py:240
  109.9 30.8 %collective-permute-start.10 = (f32[4,21,8,128]{3,2,1,0:T(8,128)S(1)}, f32[4,21,8,128]{3,2,1,0:T(8,128)S(1)}, u32[]{:S(2)}, u32[]{:S(2)}) collective-permute-start(f32[4,21,8,128]{3,2,1,0:T(8,128)S(1)} %get-tuple-element.25.own), channel_id=1, source_target_pairs={{0,32},{32,64},{64,96},{96,128},{128,160},{160,192},{192,224},{224... | collective-permute-start | bytes 1032200 | tf_op jit(solution)/shard_map/ppermute | solution.py:240
  115.0 25.8 %collective-permute-start.11 = (f32[4,21,8,128]{3,2,1,0:T(8,128)S(1)}, f32[4,21,8,128]{3,2,1,0:T(8,128)S(1)}, u32[]{:S(2)}, u32[]{:S(2)}) collective-permute-start(f32[4,21,8,128]{3,2,1,0:T(8,128)S(1)} %get-tuple-element.25.own), channel_id=1, source_target_pairs={{0,480},{32,0},{64,32},{96,64},{128,96},{160,128},{192,160},{224,1... | collective-permute-start | bytes 1032200 | tf_op jit(solution)/shard_map/ppermute | solution.py:240
  119.4 15.1 %collective-permute-start.12 = (f32[2,21,8,128]{3,2,1,0:T(8,128)S(1)}, f32[2,21,8,128]{3,2,1,0:T(8,128)S(1)}, u32[]{:S(2)}, u32[]{:S(2)}) collective-permute-start(f32[2,21,8,128]{3,2,1,0:T(8,128)S(1)} %get-tuple-element.26), channel_id=1, source_target_pairs={{0,64},{32,96},{64,128},{96,160},{128,192},{160,224},{192,256},{22... | collective-permute-start | bytes 516104 | tf_op jit(solution)/shard_map/ppermute | solution.py:240
  127.6 13.1 %collective-permute-start.13 = (f32[2,21,8,128]{3,2,1,0:T(8,128)S(1)}, f32[2,21,8,128]{3,2,1,0:T(8,128)S(1)}, u32[]{:S(2)}, u32[]{:S(2)}) collective-permute-start(f32[2,21,8,128]{3,2,1,0:T(8,128)S(1)} %get-tuple-element.27), channel_id=1, source_target_pairs={{0,448},{32,480},{64,0},{96,32},{128,64},{160,96},{192,128},{224,1... | collective-permute-start | bytes 516104 | tf_op jit(solution)/shard_map/ppermute | solution.py:240

commit v2 on v1

v2 whole, which is shorter than its diff:
```python
import jax
import jax.numpy as jnp
from jax import lax
from jax.experimental import pallas as pl
from jax.experimental.pallas import tpu as pltpu
from jax.sharding import Mesh, PartitionSpec as P

f32 = jnp.float32
B = 128
ROWS = ("pair", "side")
HIGH = lax.Precision.HIGHEST
VM = pl.BlockSpec(memory_space=pltpu.VMEM)
SM = pl.BlockSpec(memory_space=pltpu.SMEM)
PARAMS = pltpu.CompilerParams(vmem_limit_bytes=48 << 20)


def block_list(nb):
    return [(b, c) for b in range(nb) for c in range(b, nb)]


def tile_array(*lead):
    return jax.ShapeDtypeStruct(tuple(lead) + (8, B), f32)


def pack_kernel(z_ref, jac_ref, rhs_ref, own, up, down, up2, down2, parts):
    z = z_ref[0]
    segs, rows, width = jac_ref.shape
    nb = width // B
    blocks = block_list(nb)
    last = segs * len(blocks)
    for p in range(4):
        for a in range(4):
            parts[p, a, last] = jnp.zeros((8, B), f32)
    grads = []
    for s in range(segs):
        jac = jac_ref[s]
        for b in range(nb):
            info = lax.dot_general(
                jac[:, b * B:(b + 1) * B], jac[:, b * B:],
                (((0,), (0,)), ((), ())), preferred_element_type=f32)
            for c in range(b, nb):
                tile = s * len(blocks) + blocks.index((b, c))
                piece = info[:, (c - b) * B:(c - b + 1) * B].reshape(4, 4, 8, B)
                for q in range(4):
                    p = lax.rem(q + 16 - z, 4)
                    for a in range(4):
                        parts[p, a, tile] = piece[a, q]
        grads.append(jnp.dot(rhs_ref[...], jac, preferred_element_type=f32)[s:s + 1])
    p = lax.rem(16 - z, 4)
    for s in range(segs):
        for b in range(nb):
            parts[p, 0, last, pl.ds(s * nb + b, 1), :] = grads[s][:, b * B:(b + 1) * B]
    own[...] = parts[0]
    up[...] = parts[1]
    up2[...] = parts[2, 0:2]
    down2[...] = parts[2, 2:4]
    down[...] = parts[3]


def first_sum_kernel(z_ref, own, up, down, up2, down2, mine, plus, minus, far, total):
    h = lax.div(z_ref[0], 4)
    near = own[...] + up[...] + down[...]
    total[0:2] = near[0:2] + up2[...]
    total[2:4] = near[2:4] + down2[...]
    mine[...] = total[h]
    plus[...] = total[lax.rem(h + 1, 4)]
    minus[...] = total[lax.rem(h + 3, 4)]
    far[...] = total[lax.rem(h + 2, 4)]


def second_sum_kernel(decay_ref, mine, plus, minus, far, out, flat):
    total = (mine[...] + plus[...]) + (minus[...] + far[...])
    half = (total.shape[0] - 1) // 2
    for s in range(2):
        flat[s, 0:8 * half] = total[s * half:(s + 1) * half].reshape(8 * half, B)
        flat[s, 8 * half:8 * half + 4] = total[2 * half, 4 * s:4 * s + 4]
        flat[s, 8 * half + 4:] = jnp.zeros((flat.shape[1] - 8 * half - 4, B), f32)
    for t in range(out.shape[0]):
        for s in range(2):
            out[t, 3 * s:3 * s + 3] = flat[s, 3 * t:3 * t + 3]
            out[t, 6 + s:7 + s] = jnp.full((1, B), decay_ref[s], f32)


def scan_kernel(chunks, out):
    now = jnp.zeros((3, B), f32)
    for t in range(chunks.shape[0]):
        for s in range(2):
            now = chunks[t, 6 + s:7 + s] * now + chunks[t, 3 * s:3 * s + 3]
            out[s, t, 0:3] = now
            out[s, t, 3:4] = jnp.zeros((1, B), f32)


def unpack_kernel(chunks, out, flat):
    half = (out.shape[0] - 1) // 2
    for g in range(2):
        for t in range(chunks.shape[1]):
            flat[g, 3 * t:3 * t + 3] = chunks[g, t, 0:3]
        out[g * half:(g + 1) * half] = flat[g, 0:8 * half].reshape(half, 8, B)
        out[2 * half, 4 * g:4 * g + 4] = flat[g, 8 * half:8 * half + 4]


def spread(row):
    return jnp.broadcast_to(row, (8, B))


def invert_factor(rows, lane, sub):
    groups = len(rows)
    for j in range(groups):
        o = 8 * j
        top = rows[j]
        inside = (lane >= o) & (lane < o + 8)
        cols = [jnp.broadcast_to(top[:, o + m:o + m + 1], (8, B)) for m in range(8)]
        a = {(r, m): spread(cols[m][r:r + 1]) for m in range(8) for r in range(m, 8)}
        d = []
        for m in range(8):
            unit = jnp.where(lane == o + m, 1.0, 0.0)
            d.append(jnp.where(inside, unit, spread(top[m:m + 1])))
        low, rs, u = {}, [], []
        for k in range(8):
            r = lax.rsqrt(a[k, k])
            rs.append(r)
            for m in range(k + 1, 8):
                low[m, k] = a[m, k] * r
            for m in range(k + 1, 8):
                for n in range(m, 8):
                    a[n, m] = a[n, m] - low[n, k] * low[m, k]
            u.append(d[k] * r)
            for m in range(k + 1, 8):
                d[m] = d[m] - low[m, k] * u[k]
        w = [None] * 8
        for m in range(7, -1, -1):
            acc = u[m]
            for k in range(7, m, -1):
                acc = acc - low[k, m] * w[k]
            w[m] = acc * rs[m]
        for i in range(j + 1, groups):
            old = rows[i]
            new = jnp.where(inside, 0.0, old)
            for m in range(7, -1, -1):
                new = new - jnp.broadcast_to(old[:, o + m:o + m + 1], (8, B)) * w[m]
            rows[i] = new
        merged = u[0]
        for m in range(1, 8):
            merged = jnp.where(sub == m, u[m], merged)
        rows[j] = merged
    return rows


def solve_kernel(z_ref, pieces, keep, send, mat, upper, inv, vec, sol):
    z = z_ref[0]
    width = mat.shape[0]
    nb = width // B
    blocks = block_list(nb)
    nblk = len(blocks)
    lane = lax.broadcasted_iota(jnp.int32, (8, B), 1)
    sub = lax.broadcasted_iota(jnp.int32, (8, B), 0)
    row_i = lax.broadcasted_iota(jnp.int32, (B, B), 0)
    col_i = lax.broadcasted_iota(jnp.int32, (B, B), 1)
    row_w = lax.broadcasted_iota(jnp.int32, (B, width), 0)
    col_w = lax.broadcasted_iota(jnp.int32, (B, width), 1)
    vec[...] = jnp.zeros(vec.shape, f32)
    for i, (b, c) in enumerate(blocks):
        if c > b:
            mat[c * B:(c + 1) * B, b * B:(b + 1) * B] = jnp.zeros((B, B), f32)
        for h in range(pieces.shape[0]):
            for g in range(2):
                at = b * B + (2 * h + g) * 8
                mat[at:at + 8, c * B:(c + 1) * B] = pieces[h, g * nblk + i]
    for b in range(nb):
        vec[0:1, b * B:(b + 1) * B] = pieces[0, 2 * nblk, b:b + 1]

    def step(b, carry):
        at = pl.multiple_of(b * B, B)
        diag = mat[pl.ds(at, B), pl.ds(at, B)]
        rows = invert_factor([diag[8 * i:8 * i + 8] for i in range(B // 8)], lane, sub)
        left = jnp.where(col_i <= row_i, jnp.concatenate(rows, axis=0), 0.0)
        inv[b] = left
        panel = jnp.dot(left, mat[pl.ds(at, B), :], precision=HIGH, preferred_element_type=f32)
        panel = jnp.where(col_w >= row_w + at, panel, 0.0)
        upper[pl.ds(at, B), :] = panel
        y = lax.dot_general(vec[:, pl.ds(at, B)], left, (((1,), (1,)), ((), ())),
                            precision=HIGH, preferred_element_type=f32)
        sol[:, pl.ds(at, B)] = y
        vec[...] = vec[...] - jnp.dot(y, panel, precision=HIGH, preferred_element_type=f32)
        mat[...] = mat[...] - lax.dot_general(panel, panel, (((0,), (0,)), ((), ())),
                                              precision=HIGH, preferred_element_type=f32)
        return carry

    lax.fori_loop(0, nb, step, 0)

    vec[...] = jnp.zeros(vec.shape, f32)
    for b in range(nb - 1, -1, -1):
        y = sol[:, b * B:(b + 1) * B]
        if b < nb - 1:
            y = y - lax.dot_general(
                vec[:, (b + 1) * B:], upper[b * B:(b + 1) * B, (b + 1) * B:],
                (((1,), (1,)), ((), ())), precision=HIGH, preferred_element_type=f32)
        vec[:, b * B:(b + 1) * B] = jnp.dot(y, inv[b], precision=HIGH, preferred_element_type=f32)
    share = keep.shape[0] - 8
    other = z + 1 - 2 * lax.rem(z, 2)
    keep[0:share] = upper[pl.ds(pl.multiple_of(z * share, share), share), :]
    send[0:share] = upper[pl.ds(pl.multiple_of(other * share, share), share), :]
    keep[share:] = vec[...]
    send[share:] = vec[...]


def join_kernel(z_ref, keep, got, factor, state):
    share = factor.shape[1]
    s = lax.rem(z_ref[0], 2)
    factor[s] = keep[0:share]
    factor[1 - s] = got[0:share]
    first = jnp.where(s == 0, keep[share:share + 1], got[share:share + 1])
    second = jnp.where(s == 0, got[share:share + 1], keep[share:share + 1])
    state[0:1] = first
    state[1:2] = second


def shifted(value, by):
    count = lax.axis_size(ROWS)
    return lax.ppermute(value, ROWS, [(i, (i + by) % count) for i in range(count)])


def on_device(jacobian, rhs, forget, restart):
    segs, rows, width = jacobian.shape
    nb = width // B
    tiles = segs * len(block_list(nb)) + 1
    tms = lax.axis_size("tm")
    z = lax.axis_index(ROWS)
    z_now = z.astype(jnp.int32).reshape(1)
    share = width // lax.axis_size(ROWS)
    decays = forget * (1.0 - 0.2 * restart.astype(f32))

    four, two, one = tile_array(4, tiles), tile_array(2, tiles), tile_array(tiles)
    own, up, down, up2, down2 = pl.pallas_call(
        pack_kernel, out_shape=[four, four, four, two, two],
        in_specs=[SM, VM, VM], out_specs=[VM] * 5,
        scratch_shapes=[pltpu.VMEM((4, 4, tiles, 8, B), f32)],
        compiler_params=PARAMS, name="pack")(z_now, jacobian, rhs)
    up, down, up2, down2 = shifted(up, 1), shifted(down, -1), shifted(up2, 2), shifted(down2, -2)
    mine, plus, minus, far = pl.pallas_call(
        first_sum_kernel, out_shape=[one] * 4,
        in_specs=[SM] + [VM] * 5, out_specs=[VM] * 4,
        scratch_shapes=[pltpu.VMEM((4, tiles, 8, B), f32)],
        compiler_params=PARAMS, name="first_sum")(z_now, own, up, down, up2, down2)
    plus, minus, far = shifted(plus, 4), shifted(minus, -4), shifted(far, 8)
    chunks = pl.pallas_call(
        second_sum_kernel, out_shape=tile_array(tms),
        in_specs=[SM] + [VM] * 4, out_specs=VM,
        scratch_shapes=[pltpu.VMEM((2, 3 * tms, B), f32)],
        compiler_params=PARAMS, name="second_sum")(decays, mine, plus, minus, far)
    chunks = lax.all_to_all(chunks, "tm", 0, 0)
    chunks = pl.pallas_call(
        scan_kernel, out_shape=jax.ShapeDtypeStruct((2, tms, 4, B), f32), in_specs=[VM], out_specs=VM,
        compiler_params=PARAMS, name="scan")(chunks)
    chunks = lax.all_to_all(chunks.reshape(2 * tms, 4, B), ("side", "tm"), 0, 0)
    mine = pl.pallas_call(
        unpack_kernel, out_shape=one, in_specs=[VM], out_specs=VM,
        scratch_shapes=[pltpu.VMEM((2, 3 * tms, B), f32)],
        compiler_params=PARAMS, name="unpack")(chunks.reshape(2, tms, 4, B))
    pieces = lax.all_gather(mine, "pair")
    keep, send = pl.pallas_call(
        solve_kernel,
        out_shape=[jax.ShapeDtypeStruct((share + 8, width), f32)] * 2,
        in_specs=[SM, VM], out_specs=[VM] * 2,
        scratch_shapes=[
            pltpu.VMEM((width, width), f32), pltpu.VMEM((width, width), f32),
            pltpu.VMEM((nb, B, B), f32), pltpu.VMEM((8, width), f32), pltpu.VMEM((8, width), f32)],
        compiler_params=PARAMS, name="solve")(z_now, pieces)
    got = lax.ppermute(send, "side", [(0, 1), (1, 0)])
    factor, state = pl.pallas_call(
        join_kernel,
        out_shape=[jax.ShapeDtypeStruct((segs, share, width), f32), jax.ShapeDtypeStruct((segs, width), f32)],
        in_specs=[SM, VM, VM], out_specs=[VM] * 2,
        compiler_params=PARAMS, name="join")(z_now, keep, got)
    return (factor, lax.dynamic_slice_in_dim(state, z * share, share, 1))


def solution(mesh):
    count, tms = mesh.devices.shape
    paired = Mesh(mesh.devices.reshape(count // 2, 2, tms), ("pair", "side", "tm"))
    in_specs = (P("tm", ROWS, None), P("tm", ROWS), P("tm"), P("tm"))
    out_specs = (P("tm", ROWS, None), P("tm", ROWS))
    return jax.shard_map(
        on_device, mesh=paired, in_specs=in_specs, out_specs=out_specs, check_vma=False
    )
```

time: 197 us -> 156 us (0.79)
  the two profiles are of different devices: /device:TPU:1 before, /device:TPU:64 now
where the time goes in v2:
time: 156 us
  blocking collectives  60.9 us (39%)
  starting transfers between devices  40.2 us (26%)
  Pallas kernels  30.7 us (20%)
  waiting for transfers between devices  21 us (13%)
  local copies, waits for them, and re-layouts  2.45 us (2%)
    ppermute x7, starting transfers between devices, shifted(): lax.ppermute(value, ROWS, [(i, (i + by) % count) for i in range(count)])  37.5 us
    all_gather x1, blocking collectives, on_device(): pieces = lax.all_gather(mine, 'pair')  33.5 us
    pallas_call x1, Pallas kernels, on_device(): pl.pallas_call(solve_kernel, out_shape=[jax.ShapeDtypeStruct((share + 8,...  28.2 us
    ppermute x7, waiting for transfers between devices, shifted(): lax.ppermute(value, ROWS, [(i, (i + by) % count) for i in range(count)])  17.4 us
    all_to_all x1, blocking collectives, on_device(): chunks = lax.all_to_all(chunks, 'tm', 0, 0)  15 us
    all_to_all x1, blocking collectives, on_device(): chunks = lax.all_to_all(chunks.reshape(2 * tms, 4, B), ('side', 'tm'), 0, 0)  12.5 us
    ppermute x1, waiting for transfers between devices, on_device(): got = lax.ppermute(send, 'side', [(0, 1), (1, 0)])  3.59 us
  transfers between devices with their start and end apart: 8, of which 5 were waited for; matrix products, arithmetic and copies ran while one was open for 0% of the time, Pallas kernels for 0%

profile of v2, /device:TPU:64, one launch (start us, length us, event | category | flops | bytes accessed | tf_op | source)
XLA Modules:
  0.0 156.0 jit_solution(3595813686077723031)
XLA Ops:
  0.6 0.0 copy-start.1
  0.6 0.7 copy-done.1
  1.3 0.0 copy-start
  1.3 1.1 copy-done
  2.5 0.9 pack.1
  3.3 3.9 %collective-permute-start = (f32[4,21,8,128]{3,2,1,0:T(8,128)S(1)}, f32[4,21,8,128]{3,2,1,0:T(8,128)S(1)}, u32[]{:S(2)}, u32[]{:S(2)}) collective-permute-start(f32[4,21,8,128]{3,2,1,0:T(8,128)S(1)} %get-tuple-element.16), channel_id=1, source_target_pairs={{0,32},{32,64},{64,96},{96,128},{128,160},{160,192},{192,224},{224... | collective-permute-start | bytes 1032200 | tf_op jit(solution)/shard_map/ppermute | solution.py:220
  7.2 2.0 %collective-permute-start.1 = (f32[4,21,8,128]{3,2,1,0:T(8,128)S(1)}, f32[4,21,8,128]{3,2,1,0:T(8,128)S(1)}, u32[]{:S(2)}, u32[]{:S(2)}) collective-permute-start(f32[4,21,8,128]{3,2,1,0:T(8,128)S(1)} %get-tuple-element.17), channel_id=1, source_target_pairs={{0,480},{32,0},{64,32},{96,64},{128,96},{160,128},{192,160},{224,1... | collective-permute-start | bytes 1032200 | tf_op jit(solution)/shard_map/ppermute | solution.py:220
  9.2 7.6 %collective-permute-start.2 = (f32[2,21,8,128]{3,2,1,0:T(8,128)S(1)}, f32[2,21,8,128]{3,2,1,0:T(8,128)S(1)}, u32[]{:S(2)}, u32[]{:S(2)}) collective-permute-start(f32[2,21,8,128]{3,2,1,0:T(8,128)S(1)} %get-tuple-element.18), channel_id=1, source_target_pairs={{0,64},{32,96},{64,128},{96,160},{128,192},{160,224},{192,256},{22... | collective-permute-start | bytes 516104 | tf_op jit(solution)/shard_map/ppermute | solution.py:220
  16.8 3.4 %collective-permute-start.3 = (f32[2,21,8,128]{3,2,1,0:T(8,128)S(1)}, f32[2,21,8,128]{3,2,1,0:T(8,128)S(1)}, u32[]{:S(2)}, u32[]{:S(2)}) collective-permute-start(f32[2,21,8,128]{3,2,1,0:T(8,128)S(1)} %get-tuple-element.19), channel_id=1, source_target_pairs={{0,448},{32,480},{64,0},{96,32},{128,64},{160,96},{192,128},{224,1... | collective-permute-start | bytes 516104 | tf_op jit(solution)/shard_map/ppermute | solution.py:220
  20.2 3.1 %collective-permute-done.2.up2 = f32[2,21,8,128]{3,2,1,0:T(8,128)S(1)} collective-permute-done((f32[2,21,8,128]{3,2,1,0:T(8,128)S(1)}, f32[2,21,8,128]{3,2,1,0:T(8,128)S(1)}, u32[]{:S(2)}, u32[]{:S(2)}) %collective-permute-start.2) | collective-permute-done | bytes 172064 | tf_op jit(solution)/shard_map/ppermute | solution.py:220
  23.2 6.5 %collective-permute-done.3.down2 = f32[2,21,8,128]{3,2,1,0:T(8,128)S(1)} collective-permute-done((f32[2,21,8,128]{3,2,1,0:T(8,128)S(1)}, f32[2,21,8,128]{3,2,1,0:T(8,128)S(1)}, u32[]{:S(2)}, u32[]{:S(2)}) %collective-permute-start.3) | collective-permute-done | bytes 172064 | tf_op jit(solution)/shard_map/ppermute | solution.py:220
  29.7 0.0 collective-permute-done.up
  29.7 0.0 collective-permute-done.1.down
  29.7 0.1 first_sum.1
  29.9 9.1 %collective-permute-start.4 = (f32[21,8,128]{2,1,0:T(8,128)S(1)}, f32[21,8,128]{2,1,0:T(8,128)S(1)}, u32[]{:S(2)}, u32[]{:S(2)}) collective-permute-start(f32[21,8,128]{2,1,0:T(8,128)S(1)} %get-tuple-element.21), channel_id=1, source_target_pairs={{0,128},{32,160},{64,192},{96,224},{128,256},{160,288},{192,320},{... | collective-permute-start | bytes 258056 | tf_op jit(solution)/shard_map/ppermute | solution.py:220
  39.0 0.0 copy-start.2
  39.0 0.0 copy-start.3
  39.0 1.9 %collective-permute-start.5 = (f32[21,8,128]{2,1,0:T(8,128)S(1)}, f32[21,8,128]{2,1,0:T(8,128)S(1)}, u32[]{:S(2)}, u32[]{:S(2)}) collective-permute-start(f32[21,8,128]{2,1,0:T(8,128)S(1)} %get-tuple-element.22), channel_id=1, source_target_pairs={{0,384},{32,416},{64,448},{96,480},{128,0},{160,32},{192,64},{224,... | collective-permute-start | bytes 258056 | tf_op jit(solution)/shard_map/ppermute | solution.py:220
  40.9 9.7 %collective-permute-start.6 = (f32[21,8,128]{2,1,0:T(8,128)S(1)}, f32[21,8,128]{2,1,0:T(8,128)S(1)}, u32[]{:S(2)}, u32[]{:S(2)}) collective-permute-start(f32[21,8,128]{2,1,0:T(8,128)S(1)} %get-tuple-element.23), channel_id=1, source_target_pairs={{0,256},{32,288},{64,320},{96,352},{128,384},{160,416},{192,448},{... | collective-permute-start | bytes 258056 | tf_op jit(solution)/shard_map/ppermute | solution.py:220
  50.6 0.0 copy-done.2
  50.6 0.0 copy-done.3
  50.6 0.0 collective-permute-done.4.plus
  50.6 2.2 %collective-permute-done.5.minus = f32[21,8,128]{2,1,0:T(8,128)S(1)} collective-permute-done((f32[21,8,128]{2,1,0:T(8,128)S(1)}, f32[21,8,128]{2,1,0:T(8,128)S(1)}, u32[]{:S(2)}, u32[]{:S(2)}) %collective-permute-start.5) | collective-permute-done | bytes 86048 | tf_op jit(solution)/shard_map/ppermute | solution.py:220
  52.8 5.6 %collective-permute-done.6.far = f32[21,8,128]{2,1,0:T(8,128)S(1)} collective-permute-done((f32[21,8,128]{2,1,0:T(8,128)S(1)}, f32[21,8,128]{2,1,0:T(8,128)S(1)}, u32[]{:S(2)}, u32[]{:S(2)}) %collective-permute-start.6) | collective-permute-done | bytes 86048 | tf_op jit(solution)/shard_map/ppermute | solution.py:220
  58.4 0.6 second_sum.1
  59.0 15.0 %all_to_all.10.chunks = f32[32,8,128]{2,1,0:T(8,128)S(1)} all-to-all(f32[32,8,128]{2,1,0:T(8,128)S(1)} %second_sum.1), channel_id=1, replica_groups=mesh['pair'=8,'side'=2,'tm'=32] {'tm'}, dimensions={0} | all-to-all | bytes 262144 | tf_op jit(solution)/shard_map/all_to_all | solution.py:251
  74.0 0.1 scan.1
  74.1 12.5 %all_to_all.11 = f32[64,4,128]{2,1,0:T(4,128)S(1)} all-to-all(f32[64,4,128]{2,1,0:T(4,128)S(1)} %bitcast.5), channel_id=1, replica_groups=mesh['pair'=8,'side'=2,'tm'=32] {'side','tm'}, dimensions={0} | all-to-all | bytes 262144 | tf_op jit(solution)/shard_map/all_to_all | solution.py:255
  86.6 33.5 %all-gather = f32[168,8,128]{2,1,0:T(8,128)S(1)} all-gather(f32[21,8,128]{2,1,0:T(8,128)S(1)} %unpack.1), channel_id=2, replica_groups=mesh['pair'=8,'side'=2,'tm'=32] {'pair'}, dimensions={0}, use_global_device_ids=true | all-gather | bytes 774144 | tf_op jit(solution)/shard_map/all_gather | solution.py:260
  120.1 28.2 %solve.1 = (f32[40,512]{1,0:T(8,128)S(1)}, f32[40,512]{1,0:T(8,128)S(1)}) custom-call(s32[1]{0:T(128)} %bitcast.z_ref, f32[8,21,8,128]{3,2,1,0:T(8,128)S(1)} %bitcast.4), custom_call_target="tpu_custom_call" | custom-call | tf_op jit(solution)/shard_map/solve/pallas_call | solution.py:261
  148.3 2.7 %collective-permute-start.7 = (f32[40,512]{1,0:T(8,128)S(1)}, f32[40,512]{1,0:T(8,128)S(1)}, u32[]{:S(2)}, u32[]{:S(2)}) collective-permute-start(f32[40,512]{1,0:T(8,128)S(1)} %get-tuple-element.25), channel_id=1, source_target_pairs={{0,32},{32,0},{1,33},{33,1},{2,34},{34,2},{3,35},{35,3},{4,36},{36... | collective-permute-start | bytes 245768 | tf_op jit(solution)/shard_map/ppermute | solution.py:269
  151.1 3.6 %collective-permute-done.7.got = f32[40,512]{1,0:T(8,128)S(1)} collective-permute-done((f32[40,512]{1,0:T(8,128)S(1)}, f32[40,512]{1,0:T(8,128)S(1)}, u32[]{:S(2)}, u32[]{:S(2)}) %collective-permute-start.7) | collective-permute-done | bytes 81952 | tf_op jit(solution)/shard_map/ppermute | solution.py:269
  154.7 0.7 join.1
  155.3 0.6 constant_dynamic-slice_fusion
  (2 shorter events, 0.0 us)
Async XLA Ops:
  0.6 0.7 copy-start.1
  1.3 1.1 copy-start
  3.3 26.4 %collective-permute-start = (f32[4,21,8,128]{3,2,1,0:T(8,128)S(1)}, f32[4,21,8,128]{3,2,1,0:T(8,128)S(1)}, u32[]{:S(2)}, u32[]{:S(2)}) collective-permute-start(f32[4,21,8,128]{3,2,1,0:T(8,128)S(1)} %get-tuple-element.16), channel_id=1, source_target_pairs={{0,32},{32,64},{64,96},{96,128},{128,160},{160,192},{192,224},{224... | collective-permute-start | bytes 1032200 | tf_op jit(solution)/shard_map/ppermute | solution.py:220
  7.2 22.6 %collective-permute-start.1 = (f32[4,21,8,128]{3,2,1,0:T(8,128)S(1)}, f32[4,21,8,128]{3,2,1,0:T(8,128)S(1)}, u32[]{:S(2)}, u32[]{:S(2)}) collective-permute-start(f32[4,21,8,128]{3,2,1,0:T(8,128)S(1)} %get-tuple-element.17), channel_id=1, source_target_pairs={{0,480},{32,0},{64,32},{96,64},{128,96},{160,128},{192,160},{224,1... | collective-permute-start | bytes 1032200 | tf_op jit(solution)/shard_map/ppermute | solution.py:220
  9.2 14.1 %collective-permute-start.2 = (f32[2,21,8,128]{3,2,1,0:T(8,128)S(1)}, f32[2,21,8,128]{3,2,1,0:T(8,128)S(1)}, u32[]{:S(2)}, u32[]{:S(2)}) collective-permute-start(f32[2,21,8,128]{3,2,1,0:T(8,128)S(1)} %get-tuple-element.18), channel_id=1, source_target_pairs={{0,64},{32,96},{64,128},{96,160},{128,192},{160,224},{192,256},{22... | collective-permute-start | bytes 516104 | tf_op jit(solution)/shard_map/ppermute | solution.py:220
  16.8 13.0 %collective-permute-start.3 = (f32[2,21,8,128]{3,2,1,0:T(8,128)S(1)}, f32[2,21,8,128]{3,2,1,0:T(8,128)S(1)}, u32[]{:S(2)}, u32[]{:S(2)}) collective-permute-start(f32[2,21,8,128]{3,2,1,0:T(8,128)S(1)} %get-tuple-element.19), channel_id=1, source_target_pairs={{0,448},{32,480},{64,0},{96,32},{128,64},{160,96},{192,128},{224,1... | collective-permute-start | bytes 516104 | tf_op jit(solution)/shard_map/ppermute | solution.py:220
  29.9 20.7 %collective-permute-start.4 = (f32[21,8,128]{2,1,0:T(8,128)S(1)}, f32[21,8,128]{2,1,0:T(8,128)S(1)}, u32[]{:S(2)}, u32[]{:S(2)}) collective-permute-start(f32[21,8,128]{2,1,0:T(8,128)S(1)} %get-tuple-element.21), channel_id=1, source_target_pairs={{0,128},{32,160},{64,192},{96,224},{128,256},{160,288},{192,320},{... | collective-permute-start | bytes 258056 | tf_op jit(solution)/shard_map/ppermute | solution.py:220
  39.0 11.6 %copy-start.2 = (f32[2]{0:T(128)S(1)}, f32[2]{0:T(128)}, u32[]{:S(2)}) copy-start(f32[2]{0:T(128)} %param.6) | copy-start | bytes 28
  39.0 11.6 %copy-start.3 = (s32[2]{0:T(128)S(1)}, s32[2]{0:T(128)}, u32[]{:S(2)}) copy-start(s32[2]{0:T(128)} %param.7) | copy-start | bytes 28
  39.0 13.8 %collective-permute-start.5 = (f32[21,8,128]{2,1,0:T(8,128)S(1)}, f32[21,8,128]{2,1,0:T(8,128)S(1)}, u32[]{:S(2)}, u32[]{:S(2)}) collective-permute-start(f32[21,8,128]{2,1,0:T(8,128)S(1)} %get-tuple-element.22), channel_id=1, source_target_pairs={{0,384},{32,416},{64,448},{96,480},{128,0},{160,32},{192,64},{224,... | collective-permute-start | bytes 258056 | tf_op jit(solution)/shard_map/ppermute | solution.py:220
  40.9 17.5 %collective-permute-start.6 = (f32[21,8,128]{2,1,0:T(8,128)S(1)}, f32[21,8,128]{2,1,0:T(8,128)S(1)}, u32[]{:S(2)}, u32[]{:S(2)}) collective-permute-start(f32[21,8,128]{2,1,0:T(8,128)S(1)} %get-tuple-element.23), channel_id=1, source_target_pairs={{0,256},{32,288},{64,320},{96,352},{128,384},{160,416},{192,448},{... | collective-permute-start | bytes 258056 | tf_op jit(solution)/shard_map/ppermute | solution.py:220
  148.3 6.3 %collective-permute-start.7 = (f32[40,512]{1,0:T(8,128)S(1)}, f32[40,512]{1,0:T(8,128)S(1)}, u32[]{:S(2)}, u32[]{:S(2)}) collective-permute-start(f32[40,512]{1,0:T(8,128)S(1)} %get-tuple-element.25), channel_id=1, source_target_pairs={{0,32},{32,0},{1,33},{33,1},{2,34},{34,2},{3,35},{35,3},{4,36},{36... | collective-permute-start | bytes 245768 | tf_op jit(solution)/shard_map/ppermute | solution.py:269

commit v3 on v2

--- a/solution.py
+++ b/solution.py
@@ -1,3 +1,4 @@
+import functools
 import jax
 import jax.numpy as jnp
 from jax import lax
@@ -103,14 +104,24 @@
     return jnp.broadcast_to(row, (8, B))
 
 
-def invert_factor(rows, lane, sub):
+def across(value, lane):
+    return jnp.broadcast_to(value[:, lane:lane + 1], (8, B))
+
+
+def invert_factor(rows, lane, sub, jobs):
     groups = len(rows)
+    jobs = list(jobs)
+    cols = [across(rows[0], m) for m in range(8)]
     for j in range(groups):
         o = 8 * j
         top = rows[j]
+        more = j + 1 < groups
         inside = (lane >= o) & (lane < o + 8)
-        cols = [jnp.broadcast_to(top[:, o + m:o + m + 1], (8, B)) for m in range(8)]
         a = {(r, m): spread(cols[m][r:r + 1]) for m in range(8) for r in range(m, 8)}
+        if more:
+            left = [across(rows[j + 1], o + m) for m in range(8)]
+            cols = [across(rows[j + 1], o + 8 + m) for m in range(8)]
+            after = jnp.where(inside, 0.0, rows[j + 1])
         d = []
         for m in range(8):
             unit = jnp.where(lane == o + m, 1.0, 0.0)
@@ -127,23 +138,48 @@
             u.append(d[k] * r)
             for m in range(k + 1, 8):
                 d[m] = d[m] - low[m, k] * u[k]
+            if more:
+                col = left[k] * r
+                for m in range(k + 1, 8):
+                    left[m] = left[m] - col * low[m, k]
+                for m in range(8):
+                    cols[m] = cols[m] - col * spread(col[m:m + 1])
+                after = after - col * u[k]
+        if more:
+            rows[j + 1] = after
         w = [None] * 8
         for m in range(7, -1, -1):
             acc = u[m]
             for k in range(7, m, -1):
                 acc = acc - low[k, m] * w[k]
             w[m] = acc * rs[m]
-        for i in range(j + 1, groups):
+        for i in range(j + 2, groups):
             old = rows[i]
             new = jnp.where(inside, 0.0, old)
             for m in range(7, -1, -1):
-                new = new - jnp.broadcast_to(old[:, o + m:o + m + 1], (8, B)) * w[m]
+                new = new - across(old, o + m) * w[m]
             rows[i] = new
         merged = u[0]
         for m in range(1, 8):
             merged = jnp.where(sub == m, u[m], merged)
         rows[j] = merged
+        if jobs:
+            jobs.pop(0)()
+    for job in jobs:
+        job()
     return rows
+
+
+def times(x, y):
+    return jnp.dot(x, y, precision=HIGH, preferred_element_type=f32)
+
+
+def left_transposed(x, y):
+    return lax.dot_general(x, y, (((0,), (0,)), ((), ())), precision=HIGH, preferred_element_type=f32)
+
+
+def right_transposed(x, y):
+    return lax.dot_general(x, y, (((1,), (1,)), ((), ())), precision=HIGH, preferred_element_type=f32)
 
 
 def solve_kernel(z_ref, pieces, keep, send, mat, upper, inv, vec, sol):
@@ -156,12 +192,8 @@
     sub = lax.broadcasted_iota(jnp.int32, (8, B), 0)
     row_i = lax.broadcasted_iota(jnp.int32, (B, B), 0)
     col_i = lax.broadcasted_iota(jnp.int32, (B, B), 1)
-    row_w = lax.broadcasted_iota(jnp.int32, (B, width), 0)
-    col_w = lax.broadcasted_iota(jnp.int32, (B, width), 1)
     vec[...] = jnp.zeros(vec.shape, f32)
     for i, (b, c) in enumerate(blocks):
-        if c > b:
-            mat[c * B:(c + 1) * B, b * B:(b + 1) * B] = jnp.zeros((B, B), f32)
         for h in range(pieces.shape[0]):
             for g in range(2):
                 at = b * B + (2 * h + g) * 8
@@ -169,33 +201,54 @@
     for b in range(nb):
         vec[0:1, b * B:(b + 1) * B] = pieces[0, 2 * nblk, b:b + 1]
 
-    def step(b, carry):
-        at = pl.multiple_of(b * B, B)
-        diag = mat[pl.ds(at, B), pl.ds(at, B)]
-        rows = invert_factor([diag[8 * i:8 * i + 8] for i in range(B // 8)], lane, sub)
-        left = jnp.where(col_i <= row_i, jnp.concatenate(rows, axis=0), 0.0)
-        inv[b] = left
-        panel = jnp.dot(left, mat[pl.ds(at, B), :], precision=HIGH, preferred_element_type=f32)
-        panel = jnp.where(col_w >= row_w + at, panel, 0.0)
-        upper[pl.ds(at, B), :] = panel
-        y = lax.dot_general(vec[:, pl.ds(at, B)], left, (((1,), (1,)), ((), ())),
-                            precision=HIGH, preferred_element_type=f32)
-        sol[:, pl.ds(at, B)] = y
-        vec[...] = vec[...] - jnp.dot(y, panel, precision=HIGH, preferred_element_type=f32)
-        mat[...] = mat[...] - lax.dot_general(panel, panel, (((0,), (0,)), ((), ())),
-                                              precision=HIGH, preferred_element_type=f32)
-        return carry
-
-    lax.fori_loop(0, nb, step, 0)
-
-    vec[...] = jnp.zeros(vec.shape, f32)
+    def span(b):
+        return slice(b * B, (b + 1) * B)
+
+    def panel(b, c):
+        upper[span(b), span(c)] = times(inv[b], mat[span(b), span(c)])
+
+    def diagonal(b):
+        block = times(inv[b], mat[span(b), span(b)])
+        upper[span(b), span(b)] = jnp.where(col_i >= row_i, block, 0.0)
+        if b:
+            upper[span(b), 0:b * B] = jnp.zeros((B, b * B), f32)
+
+    def trail(b, c, d):
+        mat[span(c), span(d)] = mat[span(c), span(d)] - left_transposed(upper[span(b), span(c)], upper[span(b), span(d)])
+
+    def forward(b):
+        sol[:, span(b)] = right_transposed(vec[:, span(b)], inv[b])
+
+    def advance(b, c):
+        vec[:, span(c)] = vec[:, span(c)] - times(sol[:, span(b)], upper[span(b), span(c)])
+
+    jobs = []
+    for b in range(nb):
+        rows = [mat[b * B + 8 * i:b * B + 8 * i + 8, span(b)] for i in range(B // 8)]
+        rows = invert_factor(rows, lane, sub, jobs)
+        inv[b] = jnp.where(col_i <= row_i, jnp.concatenate(rows, axis=0), 0.0)
+        jobs = []
+        if b + 1 < nb:
+            panel(b, b + 1)
+            trail(b, b + 1, b + 1)
+        for c in range(b + 2, nb):
+            jobs.append(functools.partial(panel, b, c))
+        for c in range(b + 1, nb):
+            for d in range(c, nb):
+                if d > b + 1:
+                    jobs.append(functools.partial(trail, b, c, d))
+        jobs.append(functools.partial(diagonal, b))
+        jobs.append(functools.partial(forward, b))
+        for c in range(b + 1, nb):
+            jobs.append(functools.partial(advance, b, c))
+    for job in jobs:
+        job()
+
     for b in range(nb - 1, -1, -1):
-        y = sol[:, b * B:(b + 1) * B]
-        if b < nb - 1:
-            y = y - lax.dot_general(
-                vec[:, (b + 1) * B:], upper[b * B:(b + 1) * B, (b + 1) * B:],
-                (((1,), (1,)), ((), ())), precision=HIGH, preferred_element_type=f32)
-        vec[:, b * B:(b + 1) * B] = jnp.dot(y, inv[b], precision=HIGH, preferred_element_type=f32)
+        y = sol[:, span(b)]
+        if b + 1 < nb:
+            y = y - right_transposed(vec[:, (b + 1) * B:], upper[span(b), (b + 1) * B:])
+        vec[:, span(b)] = times(y, inv[b])
     share = keep.shape[0] - 8
     other = z + 1 - 2 * lax.rem(z, 2)
     keep[0:share] = upper[pl.ds(pl.multiple_of(z * share, share), share), :]
@@ -209,10 +262,11 @@
     s = lax.rem(z_ref[0], 2)
     factor[s] = keep[0:share]
     factor[1 - s] = got[0:share]
-    first = jnp.where(s == 0, keep[share:share + 1], got[share:share + 1])
-    second = jnp.where(s == 0, got[share:share + 1], keep[share:share + 1])
-    state[0:1] = first
-    state[1:2] = second
+    first = jnp.where(s == 0, keep[share:], got[share:])
+    second = jnp.where(s == 0, got[share:], keep[share:])
+    left = first.shape[1] - z_ref[0] * share
+    state[0:1] = pltpu.roll(first, left, 1)[0:1, 0:share]
+    state[1:2] = pltpu.roll(second, left, 1)[0:1, 0:share]
 
 
 def shifted(value, by):
@@ -269,10 +323,10 @@
     got = lax.ppermute(send, "side", [(0, 1), (1, 0)])
     factor, state = pl.pallas_call(
         join_kernel,
-        out_shape=[jax.ShapeDtypeStruct((segs, share, width), f32), jax.ShapeDtypeStruct((segs, width), f32)],
+        out_shape=[jax.ShapeDtypeStruct((segs, share, width), f32), jax.ShapeDtypeStruct((segs, share), f32)],
         in_specs=[SM, VM, VM], out_specs=[VM] * 2,
         compiler_params=PARAMS, name="join")(z_now, keep, got)
-    return (factor, lax.dynamic_slice_in_dim(state, z * share, share, 1))
+    return (factor, state)
 
 
 def solution(mesh):

time: 156 us -> 142 us (0.910)
  Pallas kernels: 30.7 us -> 16.4 us
    pallas_call x1, Pallas kernels: 28.2 us -> 13.9 us  [on_device(): pl.pallas_call(solve_kernel, out_shape=[jax.ShapeDtypeStruct((share + 8,...]
where the time goes in v3:
time: 142 us; the launch traced here: 141 us
  blocking collectives  61.2 us (43%)
  starting transfers between devices  40.2 us (28%)
  waiting for transfers between devices  21 us (15%)
  Pallas kernels  16.4 us (12%)
  local copies, waits for them, and re-layouts  1.82 us (1%)
    ppermute x7, starting transfers between devices, shifted(): lax.ppermute(value, ROWS, [(i, (i + by) % count) for i in range(count)])  37.5 us
    all_gather x1, blocking collectives, on_device(): pieces = lax.all_gather(mine, 'pair')  33.8 us
    ppermute x7, waiting for transfers between devices, shifted(): lax.ppermute(value, ROWS, [(i, (i + by) % count) for i in range(count)])  17.4 us
    all_to_all x1, blocking collectives, on_device(): chunks = lax.all_to_all(chunks, 'tm', 0, 0)  15 us
    pallas_call x1, Pallas kernels, on_device(): pl.pallas_call(solve_kernel, out_shape=[jax.ShapeDtypeStruct((share + 8,...  13.9 us
    all_to_all x1, blocking collectives, on_device(): chunks = lax.all_to_all(chunks.reshape(2 * tms, 4, B), ('side', 'tm'), 0, 0)  12.5 us
    ppermute x1, waiting for transfers between devices, on_device(): got = lax.ppermute(send, 'side', [(0, 1), (1, 0)])  3.58 us
  transfers between devices with their start and end apart: 8, of which 5 were waited for; matrix products, arithmetic and copies ran while one was open for 0% of the time, Pallas kernels for 0%

profile of v3, /device:TPU:64, one launch (start us, length us, event | category | flops | bytes accessed | tf_op | source)
XLA Modules:
  0.0 141.4 jit_solution(2758537082309152468)
XLA Ops:
  0.6 0.0 copy-start.1
  0.6 0.7 copy-done.1
  1.3 0.0 copy-start
  1.3 1.1 copy-done
  2.5 0.9 pack.1
  3.3 3.8 %collective-permute-start = (f32[4,21,8,128]{3,2,1,0:T(8,128)S(1)}, f32[4,21,8,128]{3,2,1,0:T(8,128)S(1)}, u32[]{:S(2)}, u32[]{:S(2)}) collective-permute-start(f32[4,21,8,128]{3,2,1,0:T(8,128)S(1)} %get-tuple-element.14), channel_id=1, source_target_pairs={{0,32},{32,64},{64,96},{96,128},{128,160},{160,192},{192,224},{224... | collective-permute-start | bytes 1032200 | tf_op jit(solution)/shard_map/ppermute | solution.py:274
  7.2 2.0 %collective-permute-start.1 = (f32[4,21,8,128]{3,2,1,0:T(8,128)S(1)}, f32[4,21,8,128]{3,2,1,0:T(8,128)S(1)}, u32[]{:S(2)}, u32[]{:S(2)}) collective-permute-start(f32[4,21,8,128]{3,2,1,0:T(8,128)S(1)} %get-tuple-element.15), channel_id=1, source_target_pairs={{0,480},{32,0},{64,32},{96,64},{128,96},{160,128},{192,160},{224,1... | collective-permute-start | bytes 1032200 | tf_op jit(solution)/shard_map/ppermute | solution.py:274
  9.2 7.6 %collective-permute-start.2 = (f32[2,21,8,128]{3,2,1,0:T(8,128)S(1)}, f32[2,21,8,128]{3,2,1,0:T(8,128)S(1)}, u32[]{:S(2)}, u32[]{:S(2)}) collective-permute-start(f32[2,21,8,128]{3,2,1,0:T(8,128)S(1)} %get-tuple-element.16), channel_id=1, source_target_pairs={{0,64},{32,96},{64,128},{96,160},{128,192},{160,224},{192,256},{22... | collective-permute-start | bytes 516104 | tf_op jit(solution)/shard_map/ppermute | solution.py:274
  16.8 3.4 %collective-permute-start.3 = (f32[2,21,8,128]{3,2,1,0:T(8,128)S(1)}, f32[2,21,8,128]{3,2,1,0:T(8,128)S(1)}, u32[]{:S(2)}, u32[]{:S(2)}) collective-permute-start(f32[2,21,8,128]{3,2,1,0:T(8,128)S(1)} %get-tuple-element.17), channel_id=1, source_target_pairs={{0,448},{32,480},{64,0},{96,32},{128,64},{160,96},{192,128},{224,1... | collective-permute-start | bytes 516104 | tf_op jit(solution)/shard_map/ppermute | solution.py:274
  20.2 3.0 %collective-permute-done.2.up2 = f32[2,21,8,128]{3,2,1,0:T(8,128)S(1)} collective-permute-done((f32[2,21,8,128]{3,2,1,0:T(8,128)S(1)}, f32[2,21,8,128]{3,2,1,0:T(8,128)S(1)}, u32[]{:S(2)}, u32[]{:S(2)}) %collective-permute-start.2) | collective-permute-done | bytes 172064 | tf_op jit(solution)/shard_map/ppermute | solution.py:274
  23.2 6.5 %collective-permute-done.3.down2 = f32[2,21,8,128]{3,2,1,0:T(8,128)S(1)} collective-permute-done((f32[2,21,8,128]{3,2,1,0:T(8,128)S(1)}, f32[2,21,8,128]{3,2,1,0:T(8,128)S(1)}, u32[]{:S(2)}, u32[]{:S(2)}) %collective-permute-start.3) | collective-permute-done | bytes 172064 | tf_op jit(solution)/shard_map/ppermute | solution.py:274
  29.7 0.0 collective-permute-done.up
  29.7 0.0 collective-permute-done.1.down
  29.7 0.1 first_sum.1
  29.9 9.1 %collective-permute-start.4 = (f32[21,8,128]{2,1,0:T(8,128)S(1)}, f32[21,8,128]{2,1,0:T(8,128)S(1)}, u32[]{:S(2)}, u32[]{:S(2)}) collective-permute-start(f32[21,8,128]{2,1,0:T(8,128)S(1)} %get-tuple-element.19), channel_id=1, source_target_pairs={{0,128},{32,160},{64,192},{96,224},{128,256},{160,288},{192,320},{... | collective-permute-start | bytes 258056 | tf_op jit(solution)/shard_map/ppermute | solution.py:274
  39.0 0.0 copy-start.2
  39.0 0.0 copy-start.3
  39.0 1.9 %collective-permute-start.5 = (f32[21,8,128]{2,1,0:T(8,128)S(1)}, f32[21,8,128]{2,1,0:T(8,128)S(1)}, u32[]{:S(2)}, u32[]{:S(2)}) collective-permute-start(f32[21,8,128]{2,1,0:T(8,128)S(1)} %get-tuple-element.20), channel_id=1, source_target_pairs={{0,384},{32,416},{64,448},{96,480},{128,0},{160,32},{192,64},{224,... | collective-permute-start | bytes 258056 | tf_op jit(solution)/shard_map/ppermute | solution.py:274
  40.9 9.6 %collective-permute-start.6 = (f32[21,8,128]{2,1,0:T(8,128)S(1)}, f32[21,8,128]{2,1,0:T(8,128)S(1)}, u32[]{:S(2)}, u32[]{:S(2)}) collective-permute-start(f32[21,8,128]{2,1,0:T(8,128)S(1)} %get-tuple-element.21), channel_id=1, source_target_pairs={{0,256},{32,288},{64,320},{96,352},{128,384},{160,416},{192,448},{... | collective-permute-start | bytes 258056 | tf_op jit(solution)/shard_map/ppermute | solution.py:274
  50.6 0.0 copy-done.2
  50.6 0.0 copy-done.3
  50.6 0.0 collective-permute-done.4.plus
  50.6 2.2 %collective-permute-done.5.minus = f32[21,8,128]{2,1,0:T(8,128)S(1)} collective-permute-done((f32[21,8,128]{2,1,0:T(8,128)S(1)}, f32[21,8,128]{2,1,0:T(8,128)S(1)}, u32[]{:S(2)}, u32[]{:S(2)}) %collective-permute-start.5) | collective-permute-done | bytes 86048 | tf_op jit(solution)/shard_map/ppermute | solution.py:274
  52.9 5.6 %collective-permute-done.6.far = f32[21,8,128]{2,1,0:T(8,128)S(1)} collective-permute-done((f32[21,8,128]{2,1,0:T(8,128)S(1)}, f32[21,8,128]{2,1,0:T(8,128)S(1)}, u32[]{:S(2)}, u32[]{:S(2)}) %collective-permute-start.6) | collective-permute-done | bytes 86048 | tf_op jit(solution)/shard_map/ppermute | solution.py:274
  58.4 0.6 second_sum.1
  59.0 15.0 %all_to_all.10.chunks = f32[32,8,128]{2,1,0:T(8,128)S(1)} all-to-all(f32[32,8,128]{2,1,0:T(8,128)S(1)} %second_sum.1), channel_id=1, replica_groups=mesh['pair'=8,'side'=2,'tm'=32] {'tm'}, dimensions={0} | all-to-all | bytes 262144 | tf_op jit(solution)/shard_map/all_to_all | solution.py:305
  74.0 0.1 scan.1
  74.1 12.5 %all_to_all.11 = f32[64,4,128]{2,1,0:T(4,128)S(1)} all-to-all(f32[64,4,128]{2,1,0:T(4,128)S(1)} %bitcast.5), channel_id=1, replica_groups=mesh['pair'=8,'side'=2,'tm'=32] {'side','tm'}, dimensions={0} | all-to-all | bytes 262144 | tf_op jit(solution)/shard_map/all_to_all | solution.py:309
  86.6 33.8 %all-gather = f32[168,8,128]{2,1,0:T(8,128)S(1)} all-gather(f32[21,8,128]{2,1,0:T(8,128)S(1)} %unpack.1), channel_id=2, replica_groups=mesh['pair'=8,'side'=2,'tm'=32] {'pair'}, dimensions={0}, use_global_device_ids=true | all-gather | bytes 774144 | tf_op jit(solution)/shard_map/all_gather | solution.py:314
  120.4 13.9 %solve.1 = (f32[40,512]{1,0:T(8,128)S(1)}, f32[40,512]{1,0:T(8,128)S(1)}) custom-call(s32[1]{0:T(128)} %bitcast.z_ref, f32[8,21,8,128]{3,2,1,0:T(8,128)S(1)} %bitcast.4), custom_call_target="tpu_custom_call" | custom-call | tf_op jit(solution)/shard_map/solve/pallas_call | solution.py:315
  134.3 2.7 %collective-permute-start.7 = (f32[40,512]{1,0:T(8,128)S(1)}, f32[40,512]{1,0:T(8,128)S(1)}, u32[]{:S(2)}, u32[]{:S(2)}) collective-permute-start(f32[40,512]{1,0:T(8,128)S(1)} %get-tuple-element.23), channel_id=1, source_target_pairs={{0,32},{32,0},{1,33},{33,1},{2,34},{34,2},{3,35},{35,3},{4,36},{36... | collective-permute-start | bytes 245768 | tf_op jit(solution)/shard_map/ppermute | solution.py:323
  137.1 3.6 %collective-permute-done.7.got = f32[40,512]{1,0:T(8,128)S(1)} collective-permute-done((f32[40,512]{1,0:T(8,128)S(1)}, f32[40,512]{1,0:T(8,128)S(1)}, u32[]{:S(2)}, u32[]{:S(2)}) %collective-permute-start.7) | collective-permute-done | bytes 81952 | tf_op jit(solution)/shard_map/ppermute | solution.py:323
  140.7 0.7 join.1
  (2 shorter events, 0.0 us)
Async XLA Ops:
  0.6 0.7 copy-start.1
  1.3 1.1 copy-start
  3.3 26.4 %collective-permute-start = (f32[4,21,8,128]{3,2,1,0:T(8,128)S(1)}, f32[4,21,8,128]{3,2,1,0:T(8,128)S(1)}, u32[]{:S(2)}, u32[]{:S(2)}) collective-permute-start(f32[4,21,8,128]{3,2,1,0:T(8,128)S(1)} %get-tuple-element.14), channel_id=1, source_target_pairs={{0,32},{32,64},{64,96},{96,128},{128,160},{160,192},{192,224},{224... | collective-permute-start | bytes 1032200 | tf_op jit(solution)/shard_map/ppermute | solution.py:274
  7.2 22.6 %collective-permute-start.1 = (f32[4,21,8,128]{3,2,1,0:T(8,128)S(1)}, f32[4,21,8,128]{3,2,1,0:T(8,128)S(1)}, u32[]{:S(2)}, u32[]{:S(2)}) collective-permute-start(f32[4,21,8,128]{3,2,1,0:T(8,128)S(1)} %get-tuple-element.15), channel_id=1, source_target_pairs={{0,480},{32,0},{64,32},{96,64},{128,96},{160,128},{192,160},{224,1... | collective-permute-start | bytes 1032200 | tf_op jit(solution)/shard_map/ppermute | solution.py:274
  9.2 14.0 %collective-permute-start.2 = (f32[2,21,8,128]{3,2,1,0:T(8,128)S(1)}, f32[2,21,8,128]{3,2,1,0:T(8,128)S(1)}, u32[]{:S(2)}, u32[]{:S(2)}) collective-permute-start(f32[2,21,8,128]{3,2,1,0:T(8,128)S(1)} %get-tuple-element.16), channel_id=1, source_target_pairs={{0,64},{32,96},{64,128},{96,160},{128,192},{160,224},{192,256},{22... | collective-permute-start | bytes 516104 | tf_op jit(solution)/shard_map/ppermute | solution.py:274
  16.8 13.0 %collective-permute-start.3 = (f32[2,21,8,128]{3,2,1,0:T(8,128)S(1)}, f32[2,21,8,128]{3,2,1,0:T(8,128)S(1)}, u32[]{:S(2)}, u32[]{:S(2)}) collective-permute-start(f32[2,21,8,128]{3,2,1,0:T(8,128)S(1)} %get-tuple-element.17), channel_id=1, source_target_pairs={{0,448},{32,480},{64,0},{96,32},{128,64},{160,96},{192,128},{224,1... | collective-permute-start | bytes 516104 | tf_op jit(solution)/shard_map/ppermute | solution.py:274
  29.9 20.7 %collective-permute-start.4 = (f32[21,8,128]{2,1,0:T(8,128)S(1)}, f32[21,8,128]{2,1,0:T(8,128)S(1)}, u32[]{:S(2)}, u32[]{:S(2)}) collective-permute-start(f32[21,8,128]{2,1,0:T(8,128)S(1)} %get-tuple-element.19), channel_id=1, source_target_pairs={{0,128},{32,160},{64,192},{96,224},{128,256},{160,288},{192,320},{... | collective-permute-start | bytes 258056 | tf_op jit(solution)/shard_map/ppermute | solution.py:274
  39.0 11.6 %copy-start.2 = (f32[2]{0:T(128)S(1)}, f32[2]{0:T(128)}, u32[]{:S(2)}) copy-start(f32[2]{0:T(128)} %param.6) | copy-start | bytes 28
  39.0 11.6 %copy-start.3 = (s32[2]{0:T(128)S(1)}, s32[2]{0:T(128)}, u32[]{:S(2)}) copy-start(s32[2]{0:T(128)} %param.7) | copy-start | bytes 28
  39.0 13.9 %collective-permute-start.5 = (f32[21,8,128]{2,1,0:T(8,128)S(1)}, f32[21,8,128]{2,1,0:T(8,128)S(1)}, u32[]{:S(2)}, u32[]{:S(2)}) collective-permute-start(f32[21,8,128]{2,1,0:T(8,128)S(1)} %get-tuple-element.20), channel_id=1, source_target_pairs={{0,384},{32,416},{64,448},{96,480},{128,0},{160,32},{192,64},{224,... | collective-permute-start | bytes 258056 | tf_op jit(solution)/shard_map/ppermute | solution.py:274
  40.9 17.5 %collective-permute-start.6 = (f32[21,8,128]{2,1,0:T(8,128)S(1)}, f32[21,8,128]{2,1,0:T(8,128)S(1)}, u32[]{:S(2)}, u32[]{:S(2)}) collective-permute-start(f32[21,8,128]{2,1,0:T(8,128)S(1)} %get-tuple-element.21), channel_id=1, source_target_pairs={{0,256},{32,288},{64,320},{96,352},{128,384},{160,416},{192,448},{... | collective-permute-start | bytes 258056 | tf_op jit(solution)/shard_map/ppermute | solution.py:274
  134.3 6.3 %collective-permute-start.7 = (f32[40,512]{1,0:T(8,128)S(1)}, f32[40,512]{1,0:T(8,128)S(1)}, u32[]{:S(2)}, u32[]{:S(2)}) collective-permute-start(f32[40,512]{1,0:T(8,128)S(1)} %get-tuple-element.23), channel_id=1, source_target_pairs={{0,32},{32,0},{1,33},{33,1},{2,34},{34,2},{3,35},{35,3},{4,36},{36... | collective-permute-start | bytes 245768 | tf_op jit(solution)/shard_map/ppermute | solution.py:323

commit v4 on v3

--- a/solution.py
+++ b/solution.py
@@ -8,7 +8,7 @@
 
 f32 = jnp.float32
 B = 128
-ROWS = ("pair", "side")
+ROWS = ("half", "quarter", "near", "side")
 HIGH = lax.Precision.HIGHEST
 VM = pl.BlockSpec(memory_space=pltpu.VMEM)
 SM = pl.BlockSpec(memory_space=pltpu.SMEM)
@@ -16,11 +16,21 @@
 
 
 def block_list(nb):
-    return [(b, c) for b in range(nb) for c in range(b, nb)]
+    return [(b, c) for b in range(nb) for c in range(b, nb) if b < nb - 1]
 
 
 def tile_array(*lead):
     return jax.ShapeDtypeStruct(tuple(lead) + (8, B), f32)
+
+
+def spare_quarter():
+    row = lax.broadcasted_iota(jnp.int32, (B, B), 0)
+    col = lax.broadcasted_iota(jnp.int32, (B, B), 1)
+    return (row >= B // 2) & (col < B // 2)
+
+
+def swap_halves(block):
+    return jnp.concatenate([block[B // 2:], block[:B // 2]], axis=0)
 
 
 def pack_kernel(z_ref, jac_ref, rhs_ref, own, up, down, up2, down2, parts):
@@ -33,15 +43,24 @@
         for a in range(4):
             parts[p, a, last] = jnp.zeros((8, B), f32)
     grads = []
+    spare = spare_quarter()
     for s in range(segs):
         jac = jac_ref[s]
-        for b in range(nb):
+        quarters = None
+        for b in range(nb - 1, -1, -1):
             info = lax.dot_general(
                 jac[:, b * B:(b + 1) * B], jac[:, b * B:],
                 (((0,), (0,)), ((), ())), preferred_element_type=f32)
+            if b == nb - 1:
+                turned = pltpu.roll(info, B // 2, 1)
+                quarters = [swap_halves(info), swap_halves(turned), turned]
+                continue
             for c in range(b, nb):
                 tile = s * len(blocks) + blocks.index((b, c))
-                piece = info[:, (c - b) * B:(c - b + 1) * B].reshape(4, 4, 8, B)
+                block = info[:, (c - b) * B:(c - b + 1) * B]
+                if c == b:
+                    block = jnp.where(spare, quarters[b], block)
+                piece = block.reshape(4, 4, 8, B)
                 for q in range(4):
                     p = lax.rem(q + 16 - z, 4)
                     for a in range(4):
@@ -69,8 +88,8 @@
     far[...] = total[lax.rem(h + 2, 4)]
 
 
-def second_sum_kernel(decay_ref, mine, plus, minus, far, out, flat):
-    total = (mine[...] + plus[...]) + (minus[...] + far[...])
+def second_sum_kernel(z_ref, decay_ref, mine, plus, minus, far, out, flat):
+    total = (mine[...] + plus[...]) + (minus[...] + far[1 - lax.div(z_ref[0], 8)])
     half = (total.shape[0] - 1) // 2
     for s in range(2):
         flat[s, 0:8 * half] = total[s * half:(s + 1) * half].reshape(8 * half, B)
@@ -222,7 +241,20 @@
     def advance(b, c):
         vec[:, span(c)] = vec[:, span(c)] - times(sol[:, span(b)], upper[span(b), span(c)])
 
-    jobs = []
+    spare = spare_quarter()
+    first, second, third = [mat[span(b), span(b)] for b in range(3)]
+    right = col_i >= B // 2
+    mat[span(3), span(3)] = jnp.where(
+        row_i < B // 2,
+        jnp.where(right, pltpu.roll(swap_halves(second), B // 2, 1), swap_halves(first)),
+        pltpu.roll(third, B // 2, 1))
+
+    def mirror(b):
+        block = mat[span(b), span(b)]
+        mat[span(b), span(b)] = jnp.where(spare, block.T, block)
+
+    mirror(0)
+    jobs = [functools.partial(mirror, b) for b in range(1, nb)]
     for b in range(nb):
         rows = [mat[b * B + 8 * i:b * B + 8 * i + 8, span(b)] for i in range(B // 8)]
         rows = invert_factor(rows, lane, sub, jobs)
@@ -296,12 +328,13 @@
         in_specs=[SM] + [VM] * 5, out_specs=[VM] * 4,
         scratch_shapes=[pltpu.VMEM((4, tiles, 8, B), f32)],
         compiler_params=PARAMS, name="first_sum")(z_now, own, up, down, up2, down2)
-    plus, minus, far = shifted(plus, 4), shifted(minus, -4), shifted(far, 8)
+    plus, minus = shifted(plus, 4), shifted(minus, -4)
+    far = lax.all_gather(far, "half")
     chunks = pl.pallas_call(
         second_sum_kernel, out_shape=tile_array(tms),
-        in_specs=[SM] + [VM] * 4, out_specs=VM,
+        in_specs=[SM, SM] + [VM] * 4, out_specs=VM,
         scratch_shapes=[pltpu.VMEM((2, 3 * tms, B), f32)],
-        compiler_params=PARAMS, name="second_sum")(decays, mine, plus, minus, far)
+        compiler_params=PARAMS, name="second_sum")(z_now, decays, mine, plus, minus, far)
     chunks = lax.all_to_all(chunks, "tm", 0, 0)
     chunks = pl.pallas_call(
         scan_kernel, out_shape=jax.ShapeDtypeStruct((2, tms, 4, B), f32), in_specs=[VM], out_specs=VM,
@@ -311,7 +344,7 @@
         unpack_kernel, out_shape=one, in_specs=[VM], out_specs=VM,
         scratch_shapes=[pltpu.VMEM((2, 3 * tms, B), f32)],
         compiler_params=PARAMS, name="unpack")(chunks.reshape(2, tms, 4, B))
-    pieces = lax.all_gather(mine, "pair")
+    pieces = lax.all_gather(mine, ("half", "quarter", "near"))
     keep, send = pl.pallas_call(
         solve_kernel,
         out_shape=[jax.ShapeDtypeStruct((share + 8, width), f32)] * 2,
@@ -331,7 +364,7 @@
 
 def solution(mesh):
     count, tms = mesh.devices.shape
-    paired = Mesh(mesh.devices.reshape(count // 2, 2, tms), ("pair", "side", "tm"))
+    paired = Mesh(mesh.devices.reshape(2, count // 8, 2, 2, tms), ROWS + ("tm",))
     in_specs = (P("tm", ROWS, None), P("tm", ROWS), P("tm"), P("tm"))
     out_specs = (P("tm", ROWS, None), P("tm", ROWS))
     return jax.shard_map(

time: 142 us -> 140 us (0.986)
  blocking collectives: 61.2 us -> 77.5 us
  starting transfers between devices: 40.2 us -> 29.7 us
  waiting for transfers between devices: 21 us -> 12.8 us
    all_gather x1 -> x2, blocking collectives: 33.8 us -> 47 us  [the longest x1 31.1 us: on_device(): pieces = lax.all_gather(mine, ('half', 'quarter', 'near'))]
    ppermute x7 -> x6, starting transfers between devices: 37.5 us -> 27.3 us  [shifted(): lax.ppermute(value, ROWS, [(i, (i + by) % count) for i in range(count)])]
    ppermute x7 -> x6, waiting for transfers between devices: 17.4 us -> 8.89 us  [shifted(): lax.ppermute(value, ROWS, [(i, (i + by) % count) for i in range(count)])]
    all_to_all x1, blocking collectives: 12.5 us -> 15.4 us  [on_device(): chunks = lax.all_to_all(chunks.reshape(2 * tms, 4, B), ('side', 'tm'), 0, 0)]
  transfers between devices with their start and end apart: 8 -> 7, of which waited for: 5 -> 3; matrix products, arithmetic and copies ran while one was open for 0% -> 0% of each run, Pallas kernels for 0% -> 0%
where the time goes in v4:
time: 140 us; the launch traced here: 139 us
  blocking collectives  77.5 us (55%)
  starting transfers between devices  29.7 us (21%)
  Pallas kernels  16.8 us (12%)
  waiting for transfers between devices  12.8 us (9%)
  local copies, waits for them, and re-layouts  1.82 us (1%)
    all_gather x1, blocking collectives, on_device(): pieces = lax.all_gather(mine, ('half', 'quarter', 'near'))  31.1 us
    ppermute x6, starting transfers between devices, shifted(): lax.ppermute(value, ROWS, [(i, (i + by) % count) for i in range(count)])  27.3 us
    all_gather x1, blocking collectives, on_device(): far = lax.all_gather(far, 'half')  15.9 us
    all_to_all x1, blocking collectives, on_device(): chunks = lax.all_to_all(chunks.reshape(2 * tms, 4, B), ('side', 'tm'), 0, 0)  15.4 us
    all_to_all x1, blocking collectives, on_device(): chunks = lax.all_to_all(chunks, 'tm', 0, 0)  15 us
    pallas_call x1, Pallas kernels, on_device(): pl.pallas_call(solve_kernel, out_shape=[jax.ShapeDtypeStruct((share + 8,...  14.4 us
    ppermute x6, waiting for transfers between devices, shifted(): lax.ppermute(value, ROWS, [(i, (i + by) % count) for i in range(count)])  8.89 us
    ppermute x1, waiting for transfers between devices, on_device(): got = lax.ppermute(send, 'side', [(0, 1), (1, 0)])  3.92 us
  transfers between devices with their start and end apart: 7, of which 3 were waited for; matrix products, arithmetic and copies ran while one was open for 0% of the time, Pallas kernels for 0%

profile of v4, /device:TPU:64, one launch (start us, length us, event | category | flops | bytes accessed | tf_op | source)
XLA Modules:
  0.0 139.4 jit_solution(17874166778462245342)
XLA Ops:
  0.6 0.0 copy-start.1
  0.7 0.7 copy-done.1
  1.3 0.0 copy-start
  1.3 1.1 copy-done
  2.5 0.9 pack.1
  3.3 3.8 %collective-permute-start = (f32[4,19,8,128]{3,2,1,0:T(8,128)S(1)}, f32[4,19,8,128]{3,2,1,0:T(8,128)S(1)}, u32[]{:S(2)}, u32[]{:S(2)}) collective-permute-start(f32[4,19,8,128]{3,2,1,0:T(8,128)S(1)} %get-tuple-element.14), channel_id=1, source_target_pairs={{0,32},{32,64},{64,96},{96,128},{128,160},{160,192},{192,224},{224... | collective-permute-start | bytes 933896 | tf_op jit(solution)/shard_map/ppermute | solution.py:306
  7.2 2.0 %collective-permute-start.1 = (f32[4,19,8,128]{3,2,1,0:T(8,128)S(1)}, f32[4,19,8,128]{3,2,1,0:T(8,128)S(1)}, u32[]{:S(2)}, u32[]{:S(2)}) collective-permute-start(f32[4,19,8,128]{3,2,1,0:T(8,128)S(1)} %get-tuple-element.15), channel_id=1, source_target_pairs={{0,480},{32,0},{64,32},{96,64},{128,96},{160,128},{192,160},{224,1... | collective-permute-start | bytes 933896 | tf_op jit(solution)/shard_map/ppermute | solution.py:306
  9.2 7.6 %collective-permute-start.2 = (f32[2,19,8,128]{3,2,1,0:T(8,128)S(1)}, f32[2,19,8,128]{3,2,1,0:T(8,128)S(1)}, u32[]{:S(2)}, u32[]{:S(2)}) collective-permute-start(f32[2,19,8,128]{3,2,1,0:T(8,128)S(1)} %get-tuple-element.16), channel_id=1, source_target_pairs={{0,64},{32,96},{64,128},{96,160},{128,192},{160,224},{192,256},{22... | collective-permute-start | bytes 466952 | tf_op jit(solution)/shard_map/ppermute | solution.py:306
  16.8 3.4 %collective-permute-start.3 = (f32[2,19,8,128]{3,2,1,0:T(8,128)S(1)}, f32[2,19,8,128]{3,2,1,0:T(8,128)S(1)}, u32[]{:S(2)}, u32[]{:S(2)}) collective-permute-start(f32[2,19,8,128]{3,2,1,0:T(8,128)S(1)} %get-tuple-element.17), channel_id=1, source_target_pairs={{0,448},{32,480},{64,0},{96,32},{128,64},{160,96},{192,128},{224,1... | collective-permute-start | bytes 466952 | tf_op jit(solution)/shard_map/ppermute | solution.py:306
  20.2 3.6 %collective-permute-done.2.up2 = f32[2,19,8,128]{3,2,1,0:T(8,128)S(1)} collective-permute-done((f32[2,19,8,128]{3,2,1,0:T(8,128)S(1)}, f32[2,19,8,128]{3,2,1,0:T(8,128)S(1)}, u32[]{:S(2)}, u32[]{:S(2)}) %collective-permute-start.2) | collective-permute-done | bytes 155680 | tf_op jit(solution)/shard_map/ppermute | solution.py:306
  23.8 5.3 %collective-permute-done.3.down2 = f32[2,19,8,128]{3,2,1,0:T(8,128)S(1)} collective-permute-done((f32[2,19,8,128]{3,2,1,0:T(8,128)S(1)}, f32[2,19,8,128]{3,2,1,0:T(8,128)S(1)}, u32[]{:S(2)}, u32[]{:S(2)}) %collective-permute-start.3) | collective-permute-done | bytes 155680 | tf_op jit(solution)/shard_map/ppermute | solution.py:306
  29.0 0.0 collective-permute-done.up
  29.0 0.0 collective-permute-done.1.down
  29.1 0.1 first_sum.1
  29.2 0.0 copy-start.2
  29.2 0.0 copy-start.3
  29.2 8.6 %collective-permute-start.4 = (f32[19,8,128]{2,1,0:T(8,128)S(1)}, f32[19,8,128]{2,1,0:T(8,128)S(1)}, u32[]{:S(2)}, u32[]{:S(2)}) collective-permute-start(f32[19,8,128]{2,1,0:T(8,128)S(1)} %get-tuple-element.19), channel_id=1, source_target_pairs={{0,128},{32,160},{64,192},{96,224},{128,256},{160,288},{192,320},{... | collective-permute-start | bytes 233480 | tf_op jit(solution)/shard_map/ppermute | solution.py:306
  37.8 1.9 %collective-permute-start.5 = (f32[19,8,128]{2,1,0:T(8,128)S(1)}, f32[19,8,128]{2,1,0:T(8,128)S(1)}, u32[]{:S(2)}, u32[]{:S(2)}) collective-permute-start(f32[19,8,128]{2,1,0:T(8,128)S(1)} %get-tuple-element.20), channel_id=1, source_target_pairs={{0,384},{32,416},{64,448},{96,480},{128,0},{160,32},{192,64},{224,... | collective-permute-start | bytes 233480 | tf_op jit(solution)/shard_map/ppermute | solution.py:306
  39.7 0.0 copy-done.2
  39.7 0.0 copy-done.3
  39.8 15.9 %all-gather = f32[38,8,128]{2,1,0:T(8,128)S(1)} all-gather(f32[19,8,128]{2,1,0:T(8,128)S(1)} %get-tuple-element.21), channel_id=2, replica_groups=mesh['half'=2,'quarter'=2,'near'=2,'side'=2,'tm'=32] {'half'}, dimensions={0}, use_global_device_ids=true | all-gather | bytes 233472 | tf_op jit(solution)/shard_map/all_gather | solution.py:332
  55.7 0.0 collective-permute-done.4.plus
  55.7 0.0 collective-permute-done.5.minus
  55.7 0.6 second_sum.1
  56.3 15.0 %all_to_all.10.chunks = f32[32,8,128]{2,1,0:T(8,128)S(1)} all-to-all(f32[32,8,128]{2,1,0:T(8,128)S(1)} %second_sum.1), channel_id=1, replica_groups=mesh['half'=2,'quarter'=2,'near'=2,'side'=2,'tm'=32] {'tm'}, dimensions={0} | all-to-all | bytes 262144 | tf_op jit(solution)/shard_map/all_to_all | solution.py:338
  71.3 0.1 scan.1
  71.5 15.4 %all_to_all.11 = f32[64,4,128]{2,1,0:T(4,128)S(1)} all-to-all(f32[64,4,128]{2,1,0:T(4,128)S(1)} %bitcast.7), channel_id=1, replica_groups=mesh['half'=2,'quarter'=2,'near'=2,'side'=2,'tm'=32] {'side','tm'}, dimensions={0} | all-to-all | bytes 262144 | tf_op jit(solution)/shard_map/all_to_all | solution.py:342
  86.9 31.1 %all-gather.1 = f32[152,8,128]{2,1,0:T(8,128)S(1)} all-gather(f32[19,8,128]{2,1,0:T(8,128)S(1)} %unpack.1), channel_id=3, replica_groups=mesh['half'=2,'quarter'=2,'near'=2,'side'=2,'tm'=32] {'half','quarter','..., dimensions={0}, use_global_device_ids=true | all-gather | bytes 700416 | tf_op jit(solution)/shard_map/all_gather | solution.py:347
  118.0 14.4 %solve.1 = (f32[40,512]{1,0:T(8,128)S(1)}, f32[40,512]{1,0:T(8,128)S(1)}) custom-call(s32[1]{0:T(128)} %bitcast.z_ref, f32[8,19,8,128]{3,2,1,0:T(8,128)S(1)} %bitcast.5), custom_call_target="tpu_custom_call" | custom-call | tf_op jit(solution)/shard_map/solve/pallas_call | solution.py:348
  132.4 2.4 %collective-permute-start.6 = (f32[40,512]{1,0:T(8,128)S(1)}, f32[40,512]{1,0:T(8,128)S(1)}, u32[]{:S(2)}, u32[]{:S(2)}) collective-permute-start(f32[40,512]{1,0:T(8,128)S(1)} %get-tuple-element.23), channel_id=1, source_target_pairs={{0,32},{32,0},{1,33},{33,1},{2,34},{34,2},{3,35},{35,3},{4,36},{36... | collective-permute-start | bytes 245768 | tf_op jit(solution)/shard_map/ppermute | solution.py:356
  134.8 3.9 %collective-permute-done.6.got = f32[40,512]{1,0:T(8,128)S(1)} collective-permute-done((f32[40,512]{1,0:T(8,128)S(1)}, f32[40,512]{1,0:T(8,128)S(1)}, u32[]{:S(2)}, u32[]{:S(2)}) %collective-permute-start.6) | collective-permute-done | bytes 81952 | tf_op jit(solution)/shard_map/ppermute | solution.py:356
  138.7 0.7 join.1
  (2 shorter events, 0.0 us)
Async XLA Ops:
  0.6 0.7 copy-start.1
  1.3 1.1 copy-start
  3.3 25.7 %collective-permute-start = (f32[4,19,8,128]{3,2,1,0:T(8,128)S(1)}, f32[4,19,8,128]{3,2,1,0:T(8,128)S(1)}, u32[]{:S(2)}, u32[]{:S(2)}) collective-permute-start(f32[4,19,8,128]{3,2,1,0:T(8,128)S(1)} %get-tuple-element.14), channel_id=1, source_target_pairs={{0,32},{32,64},{64,96},{96,128},{128,160},{160,192},{192,224},{224... | collective-permute-start | bytes 933896 | tf_op jit(solution)/shard_map/ppermute | solution.py:306
  7.2 21.9 %collective-permute-start.1 = (f32[4,19,8,128]{3,2,1,0:T(8,128)S(1)}, f32[4,19,8,128]{3,2,1,0:T(8,128)S(1)}, u32[]{:S(2)}, u32[]{:S(2)}) collective-permute-start(f32[4,19,8,128]{3,2,1,0:T(8,128)S(1)} %get-tuple-element.15), channel_id=1, source_target_pairs={{0,480},{32,0},{64,32},{96,64},{128,96},{160,128},{192,160},{224,1... | collective-permute-start | bytes 933896 | tf_op jit(solution)/shard_map/ppermute | solution.py:306
  9.2 14.6 %collective-permute-start.2 = (f32[2,19,8,128]{3,2,1,0:T(8,128)S(1)}, f32[2,19,8,128]{3,2,1,0:T(8,128)S(1)}, u32[]{:S(2)}, u32[]{:S(2)}) collective-permute-start(f32[2,19,8,128]{3,2,1,0:T(8,128)S(1)} %get-tuple-element.16), channel_id=1, source_target_pairs={{0,64},{32,96},{64,128},{96,160},{128,192},{160,224},{192,256},{22... | collective-permute-start | bytes 466952 | tf_op jit(solution)/shard_map/ppermute | solution.py:306
  16.8 12.3 %collective-permute-start.3 = (f32[2,19,8,128]{3,2,1,0:T(8,128)S(1)}, f32[2,19,8,128]{3,2,1,0:T(8,128)S(1)}, u32[]{:S(2)}, u32[]{:S(2)}) collective-permute-start(f32[2,19,8,128]{3,2,1,0:T(8,128)S(1)} %get-tuple-element.17), channel_id=1, source_target_pairs={{0,448},{32,480},{64,0},{96,32},{128,64},{160,96},{192,128},{224,1... | collective-permute-start | bytes 466952 | tf_op jit(solution)/shard_map/ppermute | solution.py:306
  29.2 10.6 %copy-start.2 = (f32[2]{0:T(128)S(1)}, f32[2]{0:T(128)}, u32[]{:S(2)}) copy-start(f32[2]{0:T(128)} %param.6) | copy-start | bytes 28
  29.2 10.5 %copy-start.3 = (s32[2]{0:T(128)S(1)}, s32[2]{0:T(128)}, u32[]{:S(2)}) copy-start(s32[2]{0:T(128)} %param.7) | copy-start | bytes 28
  29.2 26.5 %collective-permute-start.4 = (f32[19,8,128]{2,1,0:T(8,128)S(1)}, f32[19,8,128]{2,1,0:T(8,128)S(1)}, u32[]{:S(2)}, u32[]{:S(2)}) collective-permute-start(f32[19,8,128]{2,1,0:T(8,128)S(1)} %get-tuple-element.19), channel_id=1, source_target_pairs={{0,128},{32,160},{64,192},{96,224},{128,256},{160,288},{192,320},{... | collective-permute-start | bytes 233480 | tf_op jit(solution)/shard_map/ppermute | solution.py:306
  37.8 17.9 %collective-permute-start.5 = (f32[19,8,128]{2,1,0:T(8,128)S(1)}, f32[19,8,128]{2,1,0:T(8,128)S(1)}, u32[]{:S(2)}, u32[]{:S(2)}) collective-permute-start(f32[19,8,128]{2,1,0:T(8,128)S(1)} %get-tuple-element.20), channel_id=1, source_target_pairs={{0,384},{32,416},{64,448},{96,480},{128,0},{160,32},{192,64},{224,... | collective-permute-start | bytes 233480 | tf_op jit(solution)/shard_map/ppermute | solution.py:306
  132.4 6.3 %collective-permute-start.6 = (f32[40,512]{1,0:T(8,128)S(1)}, f32[40,512]{1,0:T(8,128)S(1)}, u32[]{:S(2)}, u32[]{:S(2)}) collective-permute-start(f32[40,512]{1,0:T(8,128)S(1)} %get-tuple-element.23), channel_id=1, source_target_pairs={{0,32},{32,0},{1,33},{33,1},{2,34},{34,2},{3,35},{35,3},{4,36},{36... | collective-permute-start | bytes 245768 | tf_op jit(solution)/shard_map/ppermute | solution.py:356

commit v5 on v4

--- a/solution.py
+++ b/solution.py
@@ -296,7 +296,7 @@
     factor[1 - s] = got[0:share]
     first = jnp.where(s == 0, keep[share:], got[share:])
     second = jnp.where(s == 0, got[share:], keep[share:])
-    left = first.shape[1] - z_ref[0] * share
+    left = lax.rem(first.shape[1] - z_ref[0] * share, first.shape[1])
     state[0:1] = pltpu.roll(first, left, 1)[0:1, 0:share]
     state[1:2] = pltpu.roll(second, left, 1)[0:1, 0:share]
 

time: 140 us -> 140 us (level)
  no operation moved by 1% of the time
where the time goes in v5:
time: 140 us; the launch traced here: 139 us
  blocking collectives  77.5 us (55%)
  starting transfers between devices  29.7 us (21%)
  Pallas kernels  16.8 us (12%)
  waiting for transfers between devices  12.8 us (9%)
  local copies, waits for them, and re-layouts  1.82 us (1%)
    all_gather x1, blocking collectives, on_device(): pieces = lax.all_gather(mine, ('half', 'quarter', 'near'))  31.1 us
    ppermute x6, starting transfers between devices, shifted(): lax.ppermute(value, ROWS, [(i, (i + by) % count) for i in range(count)])  27.3 us
    all_gather x1, blocking collectives, on_device(): far = lax.all_gather(far, 'half')  15.9 us
    all_to_all x1, blocking collectives, on_device(): chunks = lax.all_to_all(chunks.reshape(2 * tms, 4, B), ('side', 'tm'), 0, 0)  15.4 us
    all_to_all x1, blocking collectives, on_device(): chunks = lax.all_to_all(chunks, 'tm', 0, 0)  15 us
    pallas_call x1, Pallas kernels, on_device(): pl.pallas_call(solve_kernel, out_shape=[jax.ShapeDtypeStruct((share + 8,...  14.4 us
    ppermute x6, waiting for transfers between devices, shifted(): lax.ppermute(value, ROWS, [(i, (i + by) % count) for i in range(count)])  8.89 us
    ppermute x1, waiting for transfers between devices, on_device(): got = lax.ppermute(send, 'side', [(0, 1), (1, 0)])  3.92 us
  transfers between devices with their start and end apart: 7, of which 3 were waited for; matrix products, arithmetic and copies ran while one was open for 0% of the time, Pallas kernels for 0%

profile of v5, /device:TPU:64, one launch (start us, length us, event | category | flops | bytes accessed | tf_op | source)
XLA Modules:
  0.0 139.4 jit_solution(2806987905139453550)
XLA Ops:
  0.6 0.0 copy-start.1
  0.7 0.7 copy-done.1
  1.3 0.0 copy-start
  1.3 1.1 copy-done
  2.5 0.9 pack.1
  3.3 3.8 %collective-permute-start = (f32[4,19,8,128]{3,2,1,0:T(8,128)S(1)}, f32[4,19,8,128]{3,2,1,0:T(8,128)S(1)}, u32[]{:S(2)}, u32[]{:S(2)}) collective-permute-start(f32[4,19,8,128]{3,2,1,0:T(8,128)S(1)} %get-tuple-element.14), channel_id=1, source_target_pairs={{0,32},{32,64},{64,96},{96,128},{128,160},{160,192},{192,224},{224... | collective-permute-start | bytes 933896 | tf_op jit(solution)/shard_map/ppermute | solution.py:306
  7.2 2.0 %collective-permute-start.1 = (f32[4,19,8,128]{3,2,1,0:T(8,128)S(1)}, f32[4,19,8,128]{3,2,1,0:T(8,128)S(1)}, u32[]{:S(2)}, u32[]{:S(2)}) collective-permute-start(f32[4,19,8,128]{3,2,1,0:T(8,128)S(1)} %get-tuple-element.15), channel_id=1, source_target_pairs={{0,480},{32,0},{64,32},{96,64},{128,96},{160,128},{192,160},{224,1... | collective-permute-start | bytes 933896 | tf_op jit(solution)/shard_map/ppermute | solution.py:306
  9.2 7.6 %collective-permute-start.2 = (f32[2,19,8,128]{3,2,1,0:T(8,128)S(1)}, f32[2,19,8,128]{3,2,1,0:T(8,128)S(1)}, u32[]{:S(2)}, u32[]{:S(2)}) collective-permute-start(f32[2,19,8,128]{3,2,1,0:T(8,128)S(1)} %get-tuple-element.16), channel_id=1, source_target_pairs={{0,64},{32,96},{64,128},{96,160},{128,192},{160,224},{192,256},{22... | collective-permute-start | bytes 466952 | tf_op jit(solution)/shard_map/ppermute | solution.py:306
  16.8 3.4 %collective-permute-start.3 = (f32[2,19,8,128]{3,2,1,0:T(8,128)S(1)}, f32[2,19,8,128]{3,2,1,0:T(8,128)S(1)}, u32[]{:S(2)}, u32[]{:S(2)}) collective-permute-start(f32[2,19,8,128]{3,2,1,0:T(8,128)S(1)} %get-tuple-element.17), channel_id=1, source_target_pairs={{0,448},{32,480},{64,0},{96,32},{128,64},{160,96},{192,128},{224,1... | collective-permute-start | bytes 466952 | tf_op jit(solution)/shard_map/ppermute | solution.py:306
  20.2 3.6 %collective-permute-done.2.up2 = f32[2,19,8,128]{3,2,1,0:T(8,128)S(1)} collective-permute-done((f32[2,19,8,128]{3,2,1,0:T(8,128)S(1)}, f32[2,19,8,128]{3,2,1,0:T(8,128)S(1)}, u32[]{:S(2)}, u32[]{:S(2)}) %collective-permute-start.2) | collective-permute-done | bytes 155680 | tf_op jit(solution)/shard_map/ppermute | solution.py:306
  23.8 5.3 %collective-permute-done.3.down2 = f32[2,19,8,128]{3,2,1,0:T(8,128)S(1)} collective-permute-done((f32[2,19,8,128]{3,2,1,0:T(8,128)S(1)}, f32[2,19,8,128]{3,2,1,0:T(8,128)S(1)}, u32[]{:S(2)}, u32[]{:S(2)}) %collective-permute-start.3) | collective-permute-done | bytes 155680 | tf_op jit(solution)/shard_map/ppermute | solution.py:306
  29.0 0.0 collective-permute-done.up
  29.0 0.0 collective-permute-done.1.down
  29.1 0.1 first_sum.1
  29.2 0.0 copy-start.2
  29.2 0.0 copy-start.3
  29.2 8.6 %collective-permute-start.4 = (f32[19,8,128]{2,1,0:T(8,128)S(1)}, f32[19,8,128]{2,1,0:T(8,128)S(1)}, u32[]{:S(2)}, u32[]{:S(2)}) collective-permute-start(f32[19,8,128]{2,1,0:T(8,128)S(1)} %get-tuple-element.19), channel_id=1, source_target_pairs={{0,128},{32,160},{64,192},{96,224},{128,256},{160,288},{192,320},{... | collective-permute-start | bytes 233480 | tf_op jit(solution)/shard_map/ppermute | solution.py:306
  37.8 1.9 %collective-permute-start.5 = (f32[19,8,128]{2,1,0:T(8,128)S(1)}, f32[19,8,128]{2,1,0:T(8,128)S(1)}, u32[]{:S(2)}, u32[]{:S(2)}) collective-permute-start(f32[19,8,128]{2,1,0:T(8,128)S(1)} %get-tuple-element.20), channel_id=1, source_target_pairs={{0,384},{32,416},{64,448},{96,480},{128,0},{160,32},{192,64},{224,... | collective-permute-start | bytes 233480 | tf_op jit(solution)/shard_map/ppermute | solution.py:306
  39.7 0.0 copy-done.2
  39.7 0.0 copy-done.3
  39.8 15.9 %all-gather = f32[38,8,128]{2,1,0:T(8,128)S(1)} all-gather(f32[19,8,128]{2,1,0:T(8,128)S(1)} %get-tuple-element.21), channel_id=2, replica_groups=mesh['half'=2,'quarter'=2,'near'=2,'side'=2,'tm'=32] {'half'}, dimensions={0}, use_global_device_ids=true | all-gather | bytes 233472 | tf_op jit(solution)/shard_map/all_gather | solution.py:332
  55.7 0.0 collective-permute-done.4.plus
  55.7 0.0 collective-permute-done.5.minus
  55.7 0.6 second_sum.1
  56.3 15.0 %all_to_all.10.chunks = f32[32,8,128]{2,1,0:T(8,128)S(1)} all-to-all(f32[32,8,128]{2,1,0:T(8,128)S(1)} %second_sum.1), channel_id=1, replica_groups=mesh['half'=2,'quarter'=2,'near'=2,'side'=2,'tm'=32] {'tm'}, dimensions={0} | all-to-all | bytes 262144 | tf_op jit(solution)/shard_map/all_to_all | solution.py:338
  71.3 0.1 scan.1
  71.5 15.4 %all_to_all.11 = f32[64,4,128]{2,1,0:T(4,128)S(1)} all-to-all(f32[64,4,128]{2,1,0:T(4,128)S(1)} %bitcast.7), channel_id=1, replica_groups=mesh['half'=2,'quarter'=2,'near'=2,'side'=2,'tm'=32] {'side','tm'}, dimensions={0} | all-to-all | bytes 262144 | tf_op jit(solution)/shard_map/all_to_all | solution.py:342
  86.9 31.1 %all-gather.1 = f32[152,8,128]{2,1,0:T(8,128)S(1)} all-gather(f32[19,8,128]{2,1,0:T(8,128)S(1)} %unpack.1), channel_id=3, replica_groups=mesh['half'=2,'quarter'=2,'near'=2,'side'=2,'tm'=32] {'half','quarter','..., dimensions={0}, use_global_device_ids=true | all-gather | bytes 700416 | tf_op jit(solution)/shard_map/all_gather | solution.py:347
  118.0 14.4 %solve.1 = (f32[40,512]{1,0:T(8,128)S(1)}, f32[40,512]{1,0:T(8,128)S(1)}) custom-call(s32[1]{0:T(128)} %bitcast.z_ref, f32[8,19,8,128]{3,2,1,0:T(8,128)S(1)} %bitcast.5), custom_call_target="tpu_custom_call" | custom-call | tf_op jit(solution)/shard_map/solve/pallas_call | solution.py:348
  132.4 2.4 %collective-permute-start.6 = (f32[40,512]{1,0:T(8,128)S(1)}, f32[40,512]{1,0:T(8,128)S(1)}, u32[]{:S(2)}, u32[]{:S(2)}) collective-permute-start(f32[40,512]{1,0:T(8,128)S(1)} %get-tuple-element.23), channel_id=1, source_target_pairs={{0,32},{32,0},{1,33},{33,1},{2,34},{34,2},{3,35},{35,3},{4,36},{36... | collective-permute-start | bytes 245768 | tf_op jit(solution)/shard_map/ppermute | solution.py:356
  134.8 3.9 %collective-permute-done.6.got = f32[40,512]{1,0:T(8,128)S(1)} collective-permute-done((f32[40,512]{1,0:T(8,128)S(1)}, f32[40,512]{1,0:T(8,128)S(1)}, u32[]{:S(2)}, u32[]{:S(2)}) %collective-permute-start.6) | collective-permute-done | bytes 81952 | tf_op jit(solution)/shard_map/ppermute | solution.py:356
  138.7 0.7 join.1
  (2 shorter events, 0.0 us)
Async XLA Ops:
  0.6 0.7 copy-start.1
  1.3 1.1 copy-start
  3.3 25.7 %collective-permute-start = (f32[4,19,8,128]{3,2,1,0:T(8,128)S(1)}, f32[4,19,8,128]{3,2,1,0:T(8,128)S(1)}, u32[]{:S(2)}, u32[]{:S(2)}) collective-permute-start(f32[4,19,8,128]{3,2,1,0:T(8,128)S(1)} %get-tuple-element.14), channel_id=1, source_target_pairs={{0,32},{32,64},{64,96},{96,128},{128,160},{160,192},{192,224},{224... | collective-permute-start | bytes 933896 | tf_op jit(solution)/shard_map/ppermute | solution.py:306
  7.2 21.9 %collective-permute-start.1 = (f32[4,19,8,128]{3,2,1,0:T(8,128)S(1)}, f32[4,19,8,128]{3,2,1,0:T(8,128)S(1)}, u32[]{:S(2)}, u32[]{:S(2)}) collective-permute-start(f32[4,19,8,128]{3,2,1,0:T(8,128)S(1)} %get-tuple-element.15), channel_id=1, source_target_pairs={{0,480},{32,0},{64,32},{96,64},{128,96},{160,128},{192,160},{224,1... | collective-permute-start | bytes 933896 | tf_op jit(solution)/shard_map/ppermute | solution.py:306
  9.2 14.6 %collective-permute-start.2 = (f32[2,19,8,128]{3,2,1,0:T(8,128)S(1)}, f32[2,19,8,128]{3,2,1,0:T(8,128)S(1)}, u32[]{:S(2)}, u32[]{:S(2)}) collective-permute-start(f32[2,19,8,128]{3,2,1,0:T(8,128)S(1)} %get-tuple-element.16), channel_id=1, source_target_pairs={{0,64},{32,96},{64,128},{96,160},{128,192},{160,224},{192,256},{22... | collective-permute-start | bytes 466952 | tf_op jit(solution)/shard_map/ppermute | solution.py:306
  16.8 12.3 %collective-permute-start.3 = (f32[2,19,8,128]{3,2,1,0:T(8,128)S(1)}, f32[2,19,8,128]{3,2,1,0:T(8,128)S(1)}, u32[]{:S(2)}, u32[]{:S(2)}) collective-permute-start(f32[2,19,8,128]{3,2,1,0:T(8,128)S(1)} %get-tuple-element.17), channel_id=1, source_target_pairs={{0,448},{32,480},{64,0},{96,32},{128,64},{160,96},{192,128},{224,1... | collective-permute-start | bytes 466952 | tf_op jit(solution)/shard_map/ppermute | solution.py:306
  29.2 10.6 %copy-start.2 = (f32[2]{0:T(128)S(1)}, f32[2]{0:T(128)}, u32[]{:S(2)}) copy-start(f32[2]{0:T(128)} %param.6) | copy-start | bytes 28
  29.2 10.5 %copy-start.3 = (s32[2]{0:T(128)S(1)}, s32[2]{0:T(128)}, u32[]{:S(2)}) copy-start(s32[2]{0:T(128)} %param.7) | copy-start | bytes 28
  29.2 26.5 %collective-permute-start.4 = (f32[19,8,128]{2,1,0:T(8,128)S(1)}, f32[19,8,128]{2,1,0:T(8,128)S(1)}, u32[]{:S(2)}, u32[]{:S(2)}) collective-permute-start(f32[19,8,128]{2,1,0:T(8,128)S(1)} %get-tuple-element.19), channel_id=1, source_target_pairs={{0,128},{32,160},{64,192},{96,224},{128,256},{160,288},{192,320},{... | collective-permute-start | bytes 233480 | tf_op jit(solution)/shard_map/ppermute | solution.py:306
  37.8 17.9 %collective-permute-start.5 = (f32[19,8,128]{2,1,0:T(8,128)S(1)}, f32[19,8,128]{2,1,0:T(8,128)S(1)}, u32[]{:S(2)}, u32[]{:S(2)}) collective-permute-start(f32[19,8,128]{2,1,0:T(8,128)S(1)} %get-tuple-element.20), channel_id=1, source_target_pairs={{0,384},{32,416},{64,448},{96,480},{128,0},{160,32},{192,64},{224,... | collective-permute-start | bytes 233480 | tf_op jit(solution)/shard_map/ppermute | solution.py:306
  132.4 6.3 %collective-permute-start.6 = (f32[40,512]{1,0:T(8,128)S(1)}, f32[40,512]{1,0:T(8,128)S(1)}, u32[]{:S(2)}, u32[]{:S(2)}) collective-permute-start(f32[40,512]{1,0:T(8,128)S(1)} %get-tuple-element.23), channel_id=1, source_target_pairs={{0,32},{32,0},{1,33},{33,1},{2,34},{34,2},{3,35},{35,3},{4,36},{36... | collective-permute-start | bytes 245768 | tf_op jit(solution)/shard_map/ppermute | solution.py:356

commit v6 on v5

--- a/solution.py
+++ b/solution.py
@@ -220,11 +220,11 @@
     for b in range(nb):
         vec[0:1, b * B:(b + 1) * B] = pieces[0, 2 * nblk, b:b + 1]
 
-    def span(b):
-        return slice(b * B, (b + 1) * B)
-
-    def panel(b, c):
-        upper[span(b), span(c)] = times(inv[b], mat[span(b), span(c)])
+    def span(b, end=None):
+        return slice(b * B, (b + 1 if end is None else end) * B)
+
+    def panel(b, c, end):
+        upper[span(b), span(c, end)] = times(inv[b], mat[span(b), span(c, end)])
 
     def diagonal(b):
         block = times(inv[b], mat[span(b), span(b)])
@@ -232,14 +232,16 @@
         if b:
             upper[span(b), 0:b * B] = jnp.zeros((B, b * B), f32)
 
-    def trail(b, c, d):
-        mat[span(c), span(d)] = mat[span(c), span(d)] - left_transposed(upper[span(b), span(c)], upper[span(b), span(d)])
+    def trail(b, c, d, end):
+        mat[span(c), span(d, end)] = mat[span(c), span(d, end)] - left_transposed(
+            upper[span(b), span(c)], upper[span(b), span(d, end)])
 
     def forward(b):
         sol[:, span(b)] = right_transposed(vec[:, span(b)], inv[b])
 
-    def advance(b, c):
-        vec[:, span(c)] = vec[:, span(c)] - times(sol[:, span(b)], upper[span(b), span(c)])
+    def advance(b):
+        rest = span(b + 1, nb)
+        vec[:, rest] = vec[:, rest] - times(sol[:, span(b)], upper[span(b), rest])
 
     spare = spare_quarter()
     first, second, third = [mat[span(b), span(b)] for b in range(3)]
@@ -261,18 +263,17 @@
         inv[b] = jnp.where(col_i <= row_i, jnp.concatenate(rows, axis=0), 0.0)
         jobs = []
         if b + 1 < nb:
-            panel(b, b + 1)
-            trail(b, b + 1, b + 1)
+            panel(b, b + 1, b + 2)
+            trail(b, b + 1, b + 1, b + 2)
+        jobs.append(functools.partial(forward, b))
+        if b + 2 < nb:
+            jobs.append(functools.partial(panel, b, b + 2, nb))
+            jobs.append(functools.partial(trail, b, b + 1, b + 2, nb))
         for c in range(b + 2, nb):
-            jobs.append(functools.partial(panel, b, c))
-        for c in range(b + 1, nb):
-            for d in range(c, nb):
-                if d > b + 1:
-                    jobs.append(functools.partial(trail, b, c, d))
+            jobs.append(functools.partial(trail, b, c, c, nb))
+        if b + 1 < nb:
+            jobs.append(functools.partial(advance, b))
         jobs.append(functools.partial(diagonal, b))
-        jobs.append(functools.partial(forward, b))
-        for c in range(b + 1, nb):
-            jobs.append(functools.partial(advance, b, c))
     for job in jobs:
         job()
 

time: 140 us -> 140 us (level)
  no operation moved by 1% of the time
where the time goes in v6:
time: 140 us; the launch traced here: 139 us
  blocking collectives  77.5 us (55%)
  starting transfers between devices  29.7 us (21%)
  Pallas kernels  16.8 us (12%)
  waiting for transfers between devices  12.8 us (9%)
  local copies, waits for them, and re-layouts  1.82 us (1%)
    all_gather x1, blocking collectives, on_device(): pieces = lax.all_gather(mine, ('half', 'quarter', 'near'))  31.1 us
    ppermute x6, starting transfers between devices, shifted(): lax.ppermute(value, ROWS, [(i, (i + by) % count) for i in range(count)])  27.3 us
    all_gather x1, blocking collectives, on_device(): far = lax.all_gather(far, 'half')  15.9 us
    all_to_all x1, blocking collectives, on_device(): chunks = lax.all_to_all(chunks.reshape(2 * tms, 4, B), ('side', 'tm'), 0, 0)  15.4 us
    all_to_all x1, blocking collectives, on_device(): chunks = lax.all_to_all(chunks, 'tm', 0, 0)  15 us
    pallas_call x1, Pallas kernels, on_device(): pl.pallas_call(solve_kernel, out_shape=[jax.ShapeDtypeStruct((share + 8,...  14.3 us
    ppermute x6, waiting for transfers between devices, shifted(): lax.ppermute(value, ROWS, [(i, (i + by) % count) for i in range(count)])  8.89 us
    ppermute x1, waiting for transfers between devices, on_device(): got = lax.ppermute(send, 'side', [(0, 1), (1, 0)])  3.92 us
  transfers between devices with their start and end apart: 7, of which 3 were waited for; matrix products, arithmetic and copies ran while one was open for 0% of the time, Pallas kernels for 0%

profile of v6, /device:TPU:64, one launch (start us, length us, event | category | flops | bytes accessed | tf_op | source)
XLA Modules:
  0.0 139.3 jit_solution(15941726253731533037)
XLA Ops:
  0.6 0.0 copy-start.1
  0.7 0.7 copy-done.1
  1.3 0.0 copy-start
  1.3 1.1 copy-done
  2.5 0.9 pack.1
  3.3 3.8 %collective-permute-start = (f32[4,19,8,128]{3,2,1,0:T(8,128)S(1)}, f32[4,19,8,128]{3,2,1,0:T(8,128)S(1)}, u32[]{:S(2)}, u32[]{:S(2)}) collective-permute-start(f32[4,19,8,128]{3,2,1,0:T(8,128)S(1)} %get-tuple-element.14), channel_id=1, source_target_pairs={{0,32},{32,64},{64,96},{96,128},{128,160},{160,192},{192,224},{224... | collective-permute-start | bytes 933896 | tf_op jit(solution)/shard_map/ppermute | solution.py:307
  7.2 2.0 %collective-permute-start.1 = (f32[4,19,8,128]{3,2,1,0:T(8,128)S(1)}, f32[4,19,8,128]{3,2,1,0:T(8,128)S(1)}, u32[]{:S(2)}, u32[]{:S(2)}) collective-permute-start(f32[4,19,8,128]{3,2,1,0:T(8,128)S(1)} %get-tuple-element.15), channel_id=1, source_target_pairs={{0,480},{32,0},{64,32},{96,64},{128,96},{160,128},{192,160},{224,1... | collective-permute-start | bytes 933896 | tf_op jit(solution)/shard_map/ppermute | solution.py:307
  9.2 7.6 %collective-permute-start.2 = (f32[2,19,8,128]{3,2,1,0:T(8,128)S(1)}, f32[2,19,8,128]{3,2,1,0:T(8,128)S(1)}, u32[]{:S(2)}, u32[]{:S(2)}) collective-permute-start(f32[2,19,8,128]{3,2,1,0:T(8,128)S(1)} %get-tuple-element.16), channel_id=1, source_target_pairs={{0,64},{32,96},{64,128},{96,160},{128,192},{160,224},{192,256},{22... | collective-permute-start | bytes 466952 | tf_op jit(solution)/shard_map/ppermute | solution.py:307
  16.8 3.4 %collective-permute-start.3 = (f32[2,19,8,128]{3,2,1,0:T(8,128)S(1)}, f32[2,19,8,128]{3,2,1,0:T(8,128)S(1)}, u32[]{:S(2)}, u32[]{:S(2)}) collective-permute-start(f32[2,19,8,128]{3,2,1,0:T(8,128)S(1)} %get-tuple-element.17), channel_id=1, source_target_pairs={{0,448},{32,480},{64,0},{96,32},{128,64},{160,96},{192,128},{224,1... | collective-permute-start | bytes 466952 | tf_op jit(solution)/shard_map/ppermute | solution.py:307
  20.2 3.6 %collective-permute-done.2.up2 = f32[2,19,8,128]{3,2,1,0:T(8,128)S(1)} collective-permute-done((f32[2,19,8,128]{3,2,1,0:T(8,128)S(1)}, f32[2,19,8,128]{3,2,1,0:T(8,128)S(1)}, u32[]{:S(2)}, u32[]{:S(2)}) %collective-permute-start.2) | collective-permute-done | bytes 155680 | tf_op jit(solution)/shard_map/ppermute | solution.py:307
  23.8 5.3 %collective-permute-done.3.down2 = f32[2,19,8,128]{3,2,1,0:T(8,128)S(1)} collective-permute-done((f32[2,19,8,128]{3,2,1,0:T(8,128)S(1)}, f32[2,19,8,128]{3,2,1,0:T(8,128)S(1)}, u32[]{:S(2)}, u32[]{:S(2)}) %collective-permute-start.3) | collective-permute-done | bytes 155680 | tf_op jit(solution)/shard_map/ppermute | solution.py:307
  29.0 0.0 collective-permute-done.up
  29.0 0.0 collective-permute-done.1.down
  29.1 0.1 first_sum.1
  29.2 0.0 copy-start.2
  29.2 0.0 copy-start.3
  29.2 8.6 %collective-permute-start.4 = (f32[19,8,128]{2,1,0:T(8,128)S(1)}, f32[19,8,128]{2,1,0:T(8,128)S(1)}, u32[]{:S(2)}, u32[]{:S(2)}) collective-permute-start(f32[19,8,128]{2,1,0:T(8,128)S(1)} %get-tuple-element.19), channel_id=1, source_target_pairs={{0,128},{32,160},{64,192},{96,224},{128,256},{160,288},{192,320},{... | collective-permute-start | bytes 233480 | tf_op jit(solution)/shard_map/ppermute | solution.py:307
  37.8 1.9 %collective-permute-start.5 = (f32[19,8,128]{2,1,0:T(8,128)S(1)}, f32[19,8,128]{2,1,0:T(8,128)S(1)}, u32[]{:S(2)}, u32[]{:S(2)}) collective-permute-start(f32[19,8,128]{2,1,0:T(8,128)S(1)} %get-tuple-element.20), channel_id=1, source_target_pairs={{0,384},{32,416},{64,448},{96,480},{128,0},{160,32},{192,64},{224,... | collective-permute-start | bytes 233480 | tf_op jit(solution)/shard_map/ppermute | solution.py:307
  39.7 0.0 copy-done.2
  39.7 0.0 copy-done.3
  39.8 15.9 %all-gather = f32[38,8,128]{2,1,0:T(8,128)S(1)} all-gather(f32[19,8,128]{2,1,0:T(8,128)S(1)} %get-tuple-element.21), channel_id=2, replica_groups=mesh['half'=2,'quarter'=2,'near'=2,'side'=2,'tm'=32] {'half'}, dimensions={0}, use_global_device_ids=true | all-gather | bytes 233472 | tf_op jit(solution)/shard_map/all_gather | solution.py:333
  55.7 0.0 collective-permute-done.4.plus
  55.7 0.0 collective-permute-done.5.minus
  55.7 0.6 second_sum.1
  56.3 15.0 %all_to_all.10.chunks = f32[32,8,128]{2,1,0:T(8,128)S(1)} all-to-all(f32[32,8,128]{2,1,0:T(8,128)S(1)} %second_sum.1), channel_id=1, replica_groups=mesh['half'=2,'quarter'=2,'near'=2,'side'=2,'tm'=32] {'tm'}, dimensions={0} | all-to-all | bytes 262144 | tf_op jit(solution)/shard_map/all_to_all | solution.py:339
  71.3 0.1 scan.1
  71.5 15.4 %all_to_all.11 = f32[64,4,128]{2,1,0:T(4,128)S(1)} all-to-all(f32[64,4,128]{2,1,0:T(4,128)S(1)} %bitcast.7), channel_id=1, replica_groups=mesh['half'=2,'quarter'=2,'near'=2,'side'=2,'tm'=32] {'side','tm'}, dimensions={0} | all-to-all | bytes 262144 | tf_op jit(solution)/shard_map/all_to_all | solution.py:343
  86.9 31.1 %all-gather.1 = f32[152,8,128]{2,1,0:T(8,128)S(1)} all-gather(f32[19,8,128]{2,1,0:T(8,128)S(1)} %unpack.1), channel_id=3, replica_groups=mesh['half'=2,'quarter'=2,'near'=2,'side'=2,'tm'=32] {'half','quarter','..., dimensions={0}, use_global_device_ids=true | all-gather | bytes 700416 | tf_op jit(solution)/shard_map/all_gather | solution.py:348
  118.0 14.3 %solve.1 = (f32[40,512]{1,0:T(8,128)S(1)}, f32[40,512]{1,0:T(8,128)S(1)}) custom-call(s32[1]{0:T(128)} %bitcast.z_ref, f32[8,19,8,128]{3,2,1,0:T(8,128)S(1)} %bitcast.5), custom_call_target="tpu_custom_call" | custom-call | tf_op jit(solution)/shard_map/solve/pallas_call | solution.py:349
  132.3 2.4 %collective-permute-start.6 = (f32[40,512]{1,0:T(8,128)S(1)}, f32[40,512]{1,0:T(8,128)S(1)}, u32[]{:S(2)}, u32[]{:S(2)}) collective-permute-start(f32[40,512]{1,0:T(8,128)S(1)} %get-tuple-element.23), channel_id=1, source_target_pairs={{0,32},{32,0},{1,33},{33,1},{2,34},{34,2},{3,35},{35,3},{4,36},{36... | collective-permute-start | bytes 245768 | tf_op jit(solution)/shard_map/ppermute | solution.py:357
  134.7 3.9 %collective-permute-done.6.got = f32[40,512]{1,0:T(8,128)S(1)} collective-permute-done((f32[40,512]{1,0:T(8,128)S(1)}, f32[40,512]{1,0:T(8,128)S(1)}, u32[]{:S(2)}, u32[]{:S(2)}) %collective-permute-start.6) | collective-permute-done | bytes 81952 | tf_op jit(solution)/shard_map/ppermute | solution.py:357
  138.7 0.7 join.1
  (2 shorter events, 0.0 us)
Async XLA Ops:
  0.6 0.7 copy-start.1
  1.3 1.1 copy-start
  3.3 25.7 %collective-permute-start = (f32[4,19,8,128]{3,2,1,0:T(8,128)S(1)}, f32[4,19,8,128]{3,2,1,0:T(8,128)S(1)}, u32[]{:S(2)}, u32[]{:S(2)}) collective-permute-start(f32[4,19,8,128]{3,2,1,0:T(8,128)S(1)} %get-tuple-element.14), channel_id=1, source_target_pairs={{0,32},{32,64},{64,96},{96,128},{128,160},{160,192},{192,224},{224... | collective-permute-start | bytes 933896 | tf_op jit(solution)/shard_map/ppermute | solution.py:307
  7.2 21.9 %collective-permute-start.1 = (f32[4,19,8,128]{3,2,1,0:T(8,128)S(1)}, f32[4,19,8,128]{3,2,1,0:T(8,128)S(1)}, u32[]{:S(2)}, u32[]{:S(2)}) collective-permute-start(f32[4,19,8,128]{3,2,1,0:T(8,128)S(1)} %get-tuple-element.15), channel_id=1, source_target_pairs={{0,480},{32,0},{64,32},{96,64},{128,96},{160,128},{192,160},{224,1... | collective-permute-start | bytes 933896 | tf_op jit(solution)/shard_map/ppermute | solution.py:307
  9.2 14.6 %collective-permute-start.2 = (f32[2,19,8,128]{3,2,1,0:T(8,128)S(1)}, f32[2,19,8,128]{3,2,1,0:T(8,128)S(1)}, u32[]{:S(2)}, u32[]{:S(2)}) collective-permute-start(f32[2,19,8,128]{3,2,1,0:T(8,128)S(1)} %get-tuple-element.16), channel_id=1, source_target_pairs={{0,64},{32,96},{64,128},{96,160},{128,192},{160,224},{192,256},{22... | collective-permute-start | bytes 466952 | tf_op jit(solution)/shard_map/ppermute | solution.py:307
  16.8 12.3 %collective-permute-start.3 = (f32[2,19,8,128]{3,2,1,0:T(8,128)S(1)}, f32[2,19,8,128]{3,2,1,0:T(8,128)S(1)}, u32[]{:S(2)}, u32[]{:S(2)}) collective-permute-start(f32[2,19,8,128]{3,2,1,0:T(8,128)S(1)} %get-tuple-element.17), channel_id=1, source_target_pairs={{0,448},{32,480},{64,0},{96,32},{128,64},{160,96},{192,128},{224,1... | collective-permute-start | bytes 466952 | tf_op jit(solution)/shard_map/ppermute | solution.py:307
  29.2 10.6 %copy-start.2 = (f32[2]{0:T(128)S(1)}, f32[2]{0:T(128)}, u32[]{:S(2)}) copy-start(f32[2]{0:T(128)} %param.6) | copy-start | bytes 28
  29.2 10.5 %copy-start.3 = (s32[2]{0:T(128)S(1)}, s32[2]{0:T(128)}, u32[]{:S(2)}) copy-start(s32[2]{0:T(128)} %param.7) | copy-start | bytes 28
  29.2 26.5 %collective-permute-start.4 = (f32[19,8,128]{2,1,0:T(8,128)S(1)}, f32[19,8,128]{2,1,0:T(8,128)S(1)}, u32[]{:S(2)}, u32[]{:S(2)}) collective-permute-start(f32[19,8,128]{2,1,0:T(8,128)S(1)} %get-tuple-element.19), channel_id=1, source_target_pairs={{0,128},{32,160},{64,192},{96,224},{128,256},{160,288},{192,320},{... | collective-permute-start | bytes 233480 | tf_op jit(solution)/shard_map/ppermute | solution.py:307
  37.8 17.9 %collective-permute-start.5 = (f32[19,8,128]{2,1,0:T(8,128)S(1)}, f32[19,8,128]{2,1,0:T(8,128)S(1)}, u32[]{:S(2)}, u32[]{:S(2)}) collective-permute-start(f32[19,8,128]{2,1,0:T(8,128)S(1)} %get-tuple-element.20), channel_id=1, source_target_pairs={{0,384},{32,416},{64,448},{96,480},{128,0},{160,32},{192,64},{224,... | collective-permute-start | bytes 233480 | tf_op jit(solution)/shard_map/ppermute | solution.py:307
  132.3 6.3 %collective-permute-start.6 = (f32[40,512]{1,0:T(8,128)S(1)}, f32[40,512]{1,0:T(8,128)S(1)}, u32[]{:S(2)}, u32[]{:S(2)}) collective-permute-start(f32[40,512]{1,0:T(8,128)S(1)} %get-tuple-element.23), channel_id=1, source_target_pairs={{0,32},{32,0},{1,33},{33,1},{2,34},{34,2},{3,35},{35,3},{4,36},{36... | collective-permute-start | bytes 245768 | tf_op jit(solution)/shard_map/ppermute | solution.py:357
